TPU v7x, 32 devices: a whole 2x2x4 slice. The times are simulated.
32 devices in a mesh: gx: 4 (over y, x), gy: 8 (over z, core).
Axes of the slice: x: 2, y: 2, z: 4, core: 2. Of those that a mesh axis runs over, the one named last changes fastest.
Arguments:
- levels: int32 [8, 64, 8192], P(None, 'gx', 'gy'), may hold values from 0 to 7
- probe_bits: int32 [8, 8, 64, 8192], P(None, None, 'gx', 'gy'), may hold values from 0 to 1
Outputs:
- green: float32 [2, 8192, 64], P(None, ('gx', 'gy'))
- last_vector: float32 [8, 8, 64, 8192], P(None, None, 'gx', 'gy')
All inputs are finite; a program needn't handle non-finite values.
Results may differ from a plain program's by a relative error of at most 0.00011.
Values sent between devices are 32-bit elements; how exact they have to be, the bound alone decides.
No kernel may reach another device: no remote copies, remote signals or barrier semaphores. Data moves between devices by JAX's collectives and lax.ppermute only.
A program may use at most 128 MiB of HBM per device.

v0:
```python
import functools
import math

import jax
import jax.numpy as jnp
from jax import lax
from jax.experimental import pallas as pl
from jax.experimental.pallas import tpu as pltpu
from jax.sharding import PartitionSpec as P


STEPS = 4
LEVELS = 8
NE = 8192
NMOM = 2 * STEPS
LANES = 128
SUB = 8

disorder_width = 4.0
field_strength = 3.0
spectral_scale = 10.0
energy_edge = 0.9

F32 = jnp.float32


HOP = 2.0 / spectral_scale


def tile_view(array, lead):
    _, cols = array.shape[-2:]
    split = array.reshape(lead + (-1, SUB, cols // LANES, LANES))
    n = len(lead)
    return split.transpose(*range(n + 1), n + 2, n + 1, n + 3).reshape(lead + (-1, LANES))


def untile_view(view, shape):
    rows, cols = shape[-2:]
    split = view.reshape(-1, rows // SUB, cols // LANES, SUB, LANES)
    return split.transpose(0, 1, 3, 2, 4).reshape(shape)


class Rows:
    def __init__(self, ref, offset):
        self.ref, self.offset = ref, offset

    def __getitem__(self, index):
        if isinstance(index, tuple):
            return self.ref[(index[0] + self.offset,) + index[1:]]
        return self.ref[index + self.offset]

    def __setitem__(self, index, value):
        self.ref[(index[0] + self.offset,) + index[1:]] = value

    def rows(self, start, count):
        return self.ref.at[pl.ds(start + self.offset, count)]


def all_rows(refs):
    return tuple(Rows(ref, -n if n < STEPS else 0) for n, ref in enumerate(refs))


class Dims:
    def __init__(self, levels, bits, gx):
        self.q = bits.shape[0]
        self.pl, self.rows, self.cols = levels.shape
        self.ct = self.cols // LANES
        self.rt = self.rows // SUB
        self.width = self.cols + LANES
        self.total_rows = self.rows * gx
        self.row_tiles = self.pl * self.ct
        self.per_corner = LANES // (2 * STEPS)
        self.per_edge = LANES // STEPS
        self.corner_v = -(-STEPS * self.pl // self.per_corner)
        self.corner_tiles = self.corner_v + 1
        self.edge_v = -(-self.rows * self.pl // self.per_edge)
        self.edge_tiles = self.edge_v + -(-self.rows // self.per_edge)
        self.plan = {
            "ua": ((1, 2), (), False),
            "ub": ((3, 4), (1, 2, 3), True),
            "da": ((1, 2), (1, 2), True),
            "db": ((3,), (), False),
            "dc": ((4,), (3,), False),
        }

    def tiles(self, name):
        v_rows, o_rows, corners = self.plan[name]
        return len(v_rows) * self.row_tiles + len(o_rows) * self.ct + corners * self.corner_tiles

    def halo(self, name, k):
        return STEPS - k if name[0] == "u" else STEPS + self.rows - 1 + k

    def source(self, name, k):
        return STEPS + self.rows - k if name[0] == "u" else STEPS - 1 + k


def lanes_of(t):
    return slice(t * LANES, (t + 1) * LANES)


def to_spin(bits):
    return (2 * bits - 1).astype(F32)


def first_kernel(d, _, __, bits_ref, out_ref, scratch, sem):
    size = d.ct * SUB
    copies = [
        pltpu.make_async_copy(
            bits_ref.at[:, p, pl.ds((d.rt - 1) * size, size)], scratch.at[p], sem.at[p]
        )
        for p in range(d.pl)
    ]
    for copy in copies:
        copy.start()
    for p, copy in enumerate(copies):
        copy.wait()
        flat = scratch.at[p].reshape(d.q * size, LANES)
        for i, k in enumerate(d.plan["ua"][0]):
            for t in range(d.ct):
                bits = flat[pl.ds(t * SUB + SUB - k, d.q, stride=size), :]
                out_ref[i * d.row_tiles + p * d.ct + t] = to_spin(bits)


def fill_kernel(d, row_ref, bits_ref, levels_ref, v_ref, ons_ref, *refs):
    sends = dict(zip(("ub", "da", "db", "dc"), refs))
    right_ref, left_ref, scratch, lscratch, sem = refs[4:]
    lcopy = pltpu.make_async_copy(levels_ref, lscratch, sem.at[d.pl])
    copies = [
        pltpu.make_async_copy(bits_ref.at[:, p], scratch.at[p], sem.at[p]) for p in range(d.pl)
    ]
    lcopy.start()
    for copy in copies:
        copy.start()
    lcopy.wait()
    first_row = row_ref[0]
    for r in range(d.rt):
        for t in range(d.ct):
            level = lscratch[:, pl.ds((r * d.ct + t) * SUB, SUB), :].astype(F32)
            sub = lax.broadcasted_iota(jnp.int32, level.shape, 1)
            index = (first_row + r * SUB + sub).astype(F32)
            field = field_strength * ((index + 0.5) / d.total_rows - 0.5)
            onsite = disorder_width * (level / (LEVELS - 1) - 0.5) + field
            onsite = jnp.swapaxes(onsite * HOP, 0, 1)
            for i in range(SUB):
                ons_ref[STEPS + r * SUB + i, :, lanes_of(t)] = onsite[i]
    for p, copy in enumerate(copies):
        copy.wait()

        def block(r, _, p=p):
            for t in range(d.ct):
                start = pl.multiple_of((r * d.ct + t) * SUB, SUB)
                spins = jnp.swapaxes(to_spin(scratch[p, :, pl.ds(start, SUB), :]), 0, 1)
                v_ref[pl.ds(STEPS + r * SUB, SUB), p, :, lanes_of(t)] = spins
            return 0

        lax.fori_loop(0, d.rt, block, 0)
    lane = lax.broadcasted_iota(jnp.int32, (SUB, LANES), 1)
    low, high = lane < STEPS, lane >= LANES - STEPS

    def pack(items, ref, base, low_side):
        for at in range(0, len(items), d.per_edge):
            total = None
            for g, item in enumerate(items[at : at + d.per_edge]):
                tile = jnp.where(low if low_side else high, item(), 0.0)
                moved = pltpu.roll(tile, (STEPS * g + (0 if low_side else STEPS)) % LANES, 1)
                total = moved if total is None else total + moved
            ref[base + at // d.per_edge] = total

    for ref, t, low_side in ((right_ref, d.ct - 1, False), (left_ref, 0, True)):
        at = lanes_of(t)
        spins = [
            lambda r=r, p=p: v_ref[STEPS + r, p, :, at] for r in range(d.rows) for p in range(d.pl)
        ]
        pack(spins, ref, 0, low_side)
        onsite = [lambda r=r: ons_ref[STEPS + r, :, at] for r in range(d.rows)]
        pack(onsite, ref, d.edge_v, low_side)
    for name, ref in sends.items():
        v_rows, o_rows, _ = d.plan[name]
        for i, k in enumerate(v_rows):
            for p in range(d.pl):
                for t in range(d.ct):
                    ref[i * d.row_tiles + p * d.ct + t] = v_ref[d.source(name, k), p, :, lanes_of(t)]
        base = len(v_rows) * d.row_tiles
        for i, k in enumerate(o_rows):
            for t in range(d.ct):
                ref[base + i * d.ct + t] = ons_ref[d.source(name, k), :, lanes_of(t)]


def side_kernel(d, before_ref, after_ref, v_in, o_in, ub_in, da_in, v_ref, ons_ref, ub_ref, da_ref):
    lane = lax.broadcasted_iota(jnp.int32, (SUB, LANES), 1)
    low, high = lane < STEPS, lane >= LANES - STEPS

    def side(base, i):
        tile, g = base + i // d.per_edge, i % d.per_edge
        after = pltpu.roll(after_ref[tile], (-STEPS * g) % LANES, 1)
        before = pltpu.roll(before_ref[tile], (LANES - STEPS - STEPS * g) % LANES, 1)
        return jnp.where(low, after, jnp.where(high, before, 0.0))

    at = slice(d.cols, d.width)
    for r in range(d.rows):
        for p in range(d.pl):
            v_ref[STEPS + r, p, :, at] = side(0, r * d.pl + p)
        ons_ref[STEPS + r, :, at] = side(d.edge_v, r)
    for name, ref in (("ub", ub_ref), ("da", da_ref)):
        spins = [
            v_ref[d.source(name, k), p, :, at] for k in range(1, STEPS + 1) for p in range(d.pl)
        ]
        onsite = [ons_ref[d.source(name, k), :, at] for k in range(1, STEPS)]
        base = d.tiles(name) - d.corner_tiles
        for items, first in ((spins, base), (onsite, base + d.corner_v)):
            for start in range(0, len(items), d.per_corner):
                total = None
                for g, item in enumerate(items[start : start + d.per_corner]):
                    moved = pltpu.roll(item, (STEPS + 2 * STEPS * g) % LANES, 1)
                    total = moved if total is None else total + moved
                ref[first + start // d.per_corner] = total


def install(d, name, ref, v_ref, ons_ref):
    v_rows, o_rows, corners = d.plan[name]
    for i, k in enumerate(v_rows):
        for p in range(d.pl):
            for t in range(d.ct):
                v_ref[d.halo(name, k), p, :, lanes_of(t)] = ref[i * d.row_tiles + p * d.ct + t]
    base = len(v_rows) * d.row_tiles
    for i, k in enumerate(o_rows):
        for t in range(d.ct):
            ons_ref[d.halo(name, k), :, lanes_of(t)] = ref[base + i * d.ct + t]
    if not corners:
        return
    lane = lax.broadcasted_iota(jnp.int32, (SUB, LANES), 1)
    edge = (lane < STEPS) | (lane >= LANES - STEPS)
    at = slice(d.cols, d.width)

    def corner(first, i):
        tile, g = first + i // d.per_corner, i % d.per_corner
        moved = pltpu.roll(ref[tile], (-(STEPS + 2 * STEPS * g)) % LANES, 1)
        return jnp.where(edge, moved, 0.0)

    base = d.tiles(name) - d.corner_tiles
    for k in range(1, STEPS + 1):
        for p in range(d.pl):
            v_ref[d.halo(name, k), p, :, at] = corner(base, (k - 1) * d.pl + p)
        if k < STEPS:
            ons_ref[d.halo(name, k), :, at] = corner(base + d.corner_v, k - 1)


def row_values(d, n, at, v, ons, one_sided=False):
    source = v[n - 1]
    values = []
    for p in range(d.pl):
        x = source[at, p]
        beside = source[at - 1, p]
        if not one_sided:
            beside = beside + source[at + 1, p]
        beside = beside + pltpu.roll(x, 1, 1) + pltpu.roll(x, d.width - 1, 1)
        if p + 1 < d.pl:
            beside = beside + source[at, p + 1]
        if p > 0:
            beside = beside + source[at, p - 1]
        value = ons[at, pl.ds(p, SUB, stride=0), :] * x - HOP * beside
        values.append(0.5 * value if n == 1 else value - v[n - 2][at, p])
    return values


def one_row(d, n, at, v, ons):
    for p, value in enumerate(row_values(d, n, at, v, ons)):
        if n < STEPS:
            v[n][at, p] = value
        else:
            v[n][at - STEPS, p, :, : d.cols] = value[:, : d.cols]


def split_pair(x):
    high = x.astype(jnp.bfloat16).astype(F32)
    return high, x - high


def gram_row(d, at, v, last):
    total = None
    for p in range(d.pl):
        spin = v[0][at, p, :, : d.cols]
        halves = [split_pair(v[m][at, p, :, : d.cols]) for m in range(1, STEPS)]
        halves.append(split_pair(last(p)))
        right = [spin, spin]
        for pair in halves:
            right += list(pair)
        third = halves[STEPS - 2]
        left = [spin, third[0], third[1], third[1]]
        right = jnp.concatenate(right, 0).astype(jnp.bfloat16)
        left = jnp.concatenate(left, 0).astype(jnp.bfloat16)
        part = lax.dot_general(
            left, right, (((1,), (1,)), ((), ())), preferred_element_type=F32
        )
        total = part if total is None else total + part
    return total[: 3 * d.q]


def gram_shape(d):
    return (3 * d.q, LANES)


def add_gram(gram_ref, part):
    gram_ref[:, : part.shape[1]] += part


def packed_gram(d, gram):
    q = d.q
    zero, high, low = gram[:q], gram[q : 2 * q], gram[2 * q :]
    lane = lax.broadcasted_iota(jnp.int32, zero.shape, 1)
    with_zero = jnp.where(lane < q, zero, zero + pltpu.roll(zero, LANES - q, 1))
    with_third = high + pltpu.roll(high, LANES - q, 1) + low
    return jnp.where(lane % (2 * q) < q, with_zero, pltpu.roll(with_third, q, 1))


def interior_kernel(d, v_ref, ons, *refs):
    v, gram_ref = all_rows((v_ref,) + refs[:STEPS]), refs[STEPS]
    gram_ref[...] = jnp.zeros(gram_ref.shape, F32)
    for n in range(1, STEPS + 1):

        def step(row, _, n=n):
            at = row + STEPS
            one_row(d, n, at, v, ons)
            if n == STEPS:
                add_gram(gram_ref, gram_row(d, at, v, lambda p: v[n][row, p, :, : d.cols]))
            return 0

        lax.fori_loop(n, d.rows - n, step, 0)


def edge_rows(d):
    top = STEPS + d.rows - 1
    return [(n, top + STEPS - 1 - n - i) for n in range(STEPS - 1) for i in range(2)]


def wave_kernel(d, names, waves, *refs):
    recv = refs[: len(names)]
    refs = refs[len(names) + STEPS + 3 :]
    v = all_rows(refs[: STEPS + 1])
    ons, gram_ref, *extra = refs[STEPS + 1 :]
    for name, ref in zip(names, recv):
        install(d, name, ref, v[0], ons)

    def gram(at, last=None):
        part = gram_row(d, at, v, last or (lambda p: v[STEPS][at - STEPS, p, :, : d.cols]))
        add_gram(gram_ref, part)

    for side, k in waves:
        at_of = lambda n: STEPS + n - k if side == "u" else STEPS + d.rows - 1 - (n - k)
        for n in range(1, STEPS):
            one_row(d, n, at_of(n), v, ons)
        at = at_of(STEPS)
        if k < STEPS:
            one_row(d, STEPS, at, v, ons)
            gram(at)
        elif side == "u":
            one_row(d, STEPS, at, v, ons)
            gram(at, lambda p: v[STEPS][0, p, :, : d.cols] - HOP * v[STEPS - 1][at - 1, p, :, : d.cols])
    if ("d", STEPS - 1) in waves:
        at = STEPS + d.rows - 1
        for p, value in enumerate(row_values(d, STEPS, at, v, ons, one_sided=True)):
            v[STEPS][d.rows - 1, p, :, : d.cols] = value[:, : d.cols]
        gram(at)
    if ("u", STEPS) in waves:
        flush(d, v[STEPS], *extra)
    if ("d", STEPS - 2) in waves:
        top_ref, sem = extra
        done = d.rows - 2 - (d.rt - 1) * SUB
        copy = pltpu.make_async_copy(
            v[STEPS].rows((d.rt - 1) * SUB, done).at[:, :, :, pl.ds(0, d.cols)],
            top_ref.at[pl.ds(0, done)], sem,
        )
        copy.start()
        copy.wait()
    if ("d", STEPS - 1) in waves:
        edge_ref, eons_ref, tail_ref, packed_ref = extra
        for i, (n, at) in enumerate(edge_rows(d)):
            edge_ref[i] = v[n][at]
        for k in range(1, STEPS - 1):
            eons_ref[k - 1] = ons[d.halo("dc", k)]
        for i in range(2):
            tail_ref[i] = v[STEPS][d.rows - 2 + i, :, :, : d.cols]
        packed_ref[...] = packed_gram(d, gram_ref[...])


def transpose_tiles(d, r, p, rows, stage):
    for t in range(d.ct):
        tile = rows[:, :, lanes_of(t)]
        stage[p, :, pl.ds((r * d.ct + t) * SUB, SUB), :] = jnp.swapaxes(tile, 0, 1)


def flush(d, v4, out_ref, stage, sem):
    size = (d.rt - 1) * d.ct * SUB
    copies = []
    for p in range(d.pl):
        for r in range(d.rt - 1):
            transpose_tiles(d, r, p, v4.rows(r * SUB, SUB)[:, p], stage)
        copies.append(
            pltpu.make_async_copy(stage.at[p], out_ref.at[:, p, pl.ds(0, size)], sem.at[p])
        )
        copies[-1].start()
    for copy in copies:
        copy.wait()


def last_kernel(
    d, dc_ref, edge_ref, eons_ref, tail_ref, top_ref, _, out_ref, work, wons, rows, stage, sem, osem
):
    loads = [
        pltpu.make_async_copy(top_ref.at[pl.ds(0, SUB - 2), p], rows.at[p, pl.ds(0, SUB - 2)], sem.at[p])
        for p in range(d.pl)
    ]
    for load in loads:
        load.start()
    for n in range(STEPS - 1):
        for i in range(2):
            work[3 * n + 1 + i] = edge_ref[2 * n + i]
    for i in range(d.row_tiles):
        p, t = i // d.ct, i % d.ct
        work[0, p, :, lanes_of(t)] = dc_ref[i]
    for t in range(d.ct):
        wons[0, :, lanes_of(t)] = dc_ref[d.row_tiles + t]
    work[0, :, :, d.cols :] = jnp.zeros((d.pl, d.q, LANES), F32)
    wons[0, :, d.cols :] = jnp.zeros((d.pl, LANES), F32)
    for k in range(STEPS - 2):
        wons[STEPS - 2 - k] = eons_ref[k]
    for n in range(1, STEPS):
        base = 3 * (n - 1)
        for p in range(d.pl):
            x = work[base + 1, p]
            beside = work[base, p] + work[base + 2, p]
            beside = beside + pltpu.roll(x, 1, 1) + pltpu.roll(x, d.width - 1, 1)
            if p + 1 < d.pl:
                beside = beside + work[base + 1, p + 1]
            if p > 0:
                beside = beside + work[base + 1, p - 1]
            value = wons[n - 1, pl.ds(p, SUB, stride=0), :] * x - HOP * beside
            work[3 * n, p] = 0.5 * value if n == 1 else value - work[base - 1, p]
    copies = []
    size = d.ct * SUB
    for p in range(d.pl):
        rows[p, SUB - 2] = tail_ref[0, p]
        rows[p, SUB - 1] = tail_ref[1, p] - HOP * work[3 * STEPS - 3, p, :, : d.cols]
        loads[p].wait()
        transpose_tiles(d, 0, p, rows[p], stage)
        copies.append(pltpu.make_async_copy(
            stage.at[p], out_ref.at[:, p, pl.ds((d.rt - 1) * size, size)], osem.at[p]
        ))
        copies[-1].start()
    for copy in copies:
        copy.wait()


def green_kernel(d, sites, tables_ref, packed_ref, out_ref):
    q = d.q
    rest = packed_ref[...]
    parts = []
    for _ in range(3):
        parts.append(rest.astype(jnp.bfloat16).astype(F32))
        rest = rest - parts[-1]
    left = jnp.concatenate(parts + [jnp.zeros_like(rest)], 0).astype(jnp.bfloat16)
    column = lax.broadcasted_iota(jnp.int32, (LANES, LANES), 0)
    lane = lax.broadcasted_iota(jnp.int32, (LANES, LANES), 1)
    sub = lax.broadcasted_iota(jnp.int32, (q, LANES), 0)
    out_lane = lax.broadcasted_iota(jnp.int32, (q, LANES), 1)
    major, minor = lane // q, lane % q
    used = lane < q * q
    blocks = [2 * m for m in range(STEPS)] + [2 * m + 1 for m in range(1, STEPS + 1)]
    picks = []
    for block in blocks:
        for index in (minor, major):
            hit = (column == block * q + index) & used
            picks.append(jnp.where(hit, 1.0, 0.0).astype(jnp.bfloat16))
    wide = jnp.dot(left, jnp.concatenate(picks, 1), preferred_element_type=F32)
    wide = wide[:q] + wide[q : 2 * q] + wide[2 * q : 3 * q]
    straight, turned = sub == out_lane // q, sub == out_lane % q
    flat = []
    for i in range(len(blocks)):
        one = jnp.where(straight, wide[:, lanes_of(2 * i)], 0.0)
        two = jnp.where(turned, wide[:, lanes_of(2 * i + 1)], 0.0)
        flat.append(jnp.sum(one + two, 0, keepdims=True) * (0.5 / sites))
    moments = flat[:STEPS]
    for m, base in ((0, 2), (1, 1), (2, 0), (3, 1)):
        moments.append(2.0 * flat[STEPS + m] - moments[base])
    moments = jnp.concatenate(moments, 0)
    total = lax.dot_general(
        moments, tables_ref[...], (((0,), (0,)), ((), ())),
        precision=lax.Precision.HIGHEST, preferred_element_type=F32,
    )
    energies = total.shape[1] // 2
    for part in range(2):
        out_ref[part] = total[: q * q, part * energies : (part + 1) * energies]


def jackson_weights(count):
    total = count + 1.0
    values = []
    for order in range(count):
        damping = (
            (count - order + 1.0) * math.cos(math.pi * order / total)
            + math.sin(math.pi * order / total) / math.tan(math.pi / total)
        ) / total
        values.append(damping if order == 0 else 2.0 * damping)
    return jnp.asarray(values, dtype=F32)


def energy_tables(energy_index, count, total_energies):
    phase = math.pi * (energy_index.astype(F32) + 0.5) / total_energies
    theta = jnp.arccos(energy_edge * jnp.cos(phase))
    orders = jnp.arange(count).astype(F32)
    weights = jackson_weights(count)
    angles = orders[:, None] * theta[None, :]
    denominator = jnp.sin(theta)[None, :]
    real_part = -weights[:, None] * jnp.sin(angles) / denominator
    imag_part = -weights[:, None] * jnp.cos(angles) / denominator
    return jnp.concatenate([real_part, imag_part], 1)


def add_over(value, axis):
    peers = lax.axis_size(axis)
    if peers & (peers - 1):
        return lax.psum(value, axis)
    if peers == 4:
        others = [lax.ppermute(value, axis, [(i, i ^ s) for i in range(peers)]) for s in (1, 2, 3)]
        return (value + others[0]) + (others[1] + others[2])
    shift = 1
    while shift < peers:
        value = value + lax.ppermute(value, axis, [(i, i ^ shift) for i in range(peers)])
        shift *= 2
    return value


VMEM = pl.BlockSpec(memory_space=pltpu.VMEM)
SMEM = pl.BlockSpec(memory_space=pltpu.SMEM)
HBM = pl.BlockSpec(memory_space=pltpu.MemorySpace.HBM)


def params(mib):
    return pltpu.CompilerParams(vmem_limit_bytes=mib * 2**20)


def send(array, axis, step):
    peers = lax.axis_size(axis)
    return lax.ppermute(array, axis, [(i, (i + step) % peers) for i in range(peers)])


def on_device(levels, probe_bits):
    count_gx = lax.axis_size("gx")
    count_gy = lax.axis_size("gy")
    d = Dims(levels, probe_bits, count_gx)
    sites = d.pl * d.total_rows * d.cols * count_gy
    first_row = (lax.axis_index("gx") * d.rows).astype(jnp.int32).reshape(1)
    in_hbm = lambda x: pltpu.with_memory_space_constraint(x, pltpu.MemorySpace.HBM)
    per_device = NE // (count_gx * count_gy)
    first_energy = (lax.axis_index("gx") * count_gy + lax.axis_index("gy")) * per_device
    first_energy = first_energy.astype(jnp.int32).reshape(1)
    bits = tile_view(probe_bits, (d.q, d.pl))
    levels = in_hbm(tile_view(levels, (d.pl,)))
    dma = pltpu.SemaphoreType.DMA
    padded = d.rows + 2 * STEPS
    vectors = [pltpu.VMEM((padded - 2 * n, d.pl, d.q, d.width), F32) for n in range(STEPS)]
    last = pltpu.VMEM((d.rows, d.pl, d.q, d.cols), F32)
    onsite = pltpu.VMEM((padded, d.pl, d.width), F32)
    gram_type = pltpu.VMEM(gram_shape(d), F32)
    tiles = lambda n: pltpu.VMEM((n, SUB, LANES), F32)

    ua = pl.pallas_call(
        functools.partial(first_kernel, d),
        out_shape=tiles(d.tiles("ua")), in_specs=[SMEM, SMEM, HBM], out_specs=VMEM,
        scratch_shapes=[pltpu.VMEM((d.pl, d.q, d.ct * SUB, LANES), jnp.int32), dma((d.pl,))],
        compiler_params=params(4), name="first",
    )(first_row, first_energy, in_hbm(bits))
    ua = send(ua, "gx", 1)
    names = ("ub", "da", "db", "dc")
    v0, ons, *sends, right, left = pl.pallas_call(
        functools.partial(fill_kernel, d),
        out_shape=[vectors[0], onsite] + [tiles(d.tiles(name)) for name in names]
        + [tiles(d.edge_tiles)] * 2,
        in_specs=[SMEM, HBM, HBM], out_specs=[VMEM] * 8,
        scratch_shapes=[
            pltpu.VMEM((d.pl, d.q) + bits.shape[2:], jnp.int32), pltpu.VMEM(levels.shape, jnp.int32),
            dma((d.pl + 1,)),
        ],
        compiler_params=params(6), name="fill",
    )(first_row, in_hbm(bits), levels)
    ub, da, db, dc = sends
    before = send(right, "gy", 1)
    after = send(left, "gy", -1)
    v0, ons, ub, da = pl.pallas_call(
        functools.partial(side_kernel, d),
        out_shape=[vectors[0], onsite, tiles(d.tiles("ub")), tiles(d.tiles("da"))],
        in_specs=[VMEM] * 6, out_specs=[VMEM] * 4,
        input_output_aliases={2: 0, 3: 1, 4: 2, 5: 3},
        compiler_params=params(2), name="side",
    )(before, after, v0, ons, ub, da)
    ub = send(ub, "gx", 1)
    da = send(da, "gx", -1)
    db = send(db, "gx", -1)
    dc = send(dc, "gx", -1)
    *rest, gram = pl.pallas_call(
        functools.partial(interior_kernel, d),
        out_shape=vectors[1:] + [last, gram_type], in_specs=[VMEM] * 2, out_specs=[VMEM] * (STEPS + 1),
        compiler_params=params(3), name="interior",
    )(v0, ons)
    kept = [v0] + rest + [ons, gram]
    kinds = vectors + [last, onsite, gram_type]

    def wave(received, names, waves, kept, extra=(), specs=(), scratch=()):
        return pl.pallas_call(
            functools.partial(wave_kernel, d, names, waves),
            out_shape=kinds + list(extra), in_specs=[VMEM] * (len(names) + len(kept)),
            out_specs=[VMEM] * len(kept) + list(specs), scratch_shapes=list(scratch),
            input_output_aliases={len(names) + i: i for i in range(len(kept))},
            compiler_params=params(4),
        )(*received, *kept)

    every = tuple(("u", k) for k in range(1, STEPS + 1))
    stage_rows = (d.rt - 1) * d.ct * SUB
    *kept, lower = wave(
        [ua, ub], ("ua", "ub"), every, kept, [pltpu.HBM(bits.shape, F32)], [HBM],
        [pltpu.VMEM((d.pl, d.q, stage_rows, LANES), F32), dma((d.pl,))],
    )
    block = (SUB, d.pl, d.q, d.cols)
    *kept, top = wave(
        [da], ("da",), (("d", 1), ("d", 2)), kept,
        [pltpu.HBM(block, F32)], [HBM], [dma],
    )
    extra = [
        pltpu.VMEM((2 * (STEPS - 1), d.pl, d.q, d.width), F32),
        pltpu.VMEM((STEPS - 2, d.pl, d.width), F32),
        pltpu.VMEM((2,) + block[1:], F32),
        pltpu.VMEM((d.q, LANES), F32),
    ]
    *_, edge, edge_ons, tail, gram = wave([db], ("db",), (("d", 3),), kept, extra, [VMEM] * 4)
    last_vector = pl.pallas_call(
        functools.partial(last_kernel, d),
        out_shape=jax.ShapeDtypeStruct(bits.shape, F32),
        in_specs=[VMEM] * 4 + [HBM] * 2, out_specs=HBM,
        scratch_shapes=[
            pltpu.VMEM((3 * STEPS - 2, d.pl, d.q, d.width), F32),
            pltpu.VMEM((STEPS - 1, d.pl, d.width), F32),
            pltpu.VMEM((d.pl, SUB, d.q, d.cols), F32),
            pltpu.VMEM((d.pl, d.q, d.ct * SUB, LANES), F32), dma((d.pl,)), dma((d.pl,)),
        ],
        input_output_aliases={5: 0},
        compiler_params=params(9), name="last",
    )(dc, edge, edge_ons, tail, top, lower)
    last_vector = untile_view(last_vector, probe_bits.shape)

    gram = add_over(add_over(gram, "gy"), "gx")
    tables = energy_tables(first_energy + jnp.arange(per_device), NMOM, NE)
    green = pl.pallas_call(
        functools.partial(green_kernel, d, sites),
        out_shape=jax.ShapeDtypeStruct((2, d.q * d.q, per_device), F32),
        in_specs=[VMEM] * 2, out_specs=VMEM, compiler_params=params(2), name="green",
    )(tables, gram)
    return green.transpose(0, 2, 1), last_vector


def solution(mesh):
    placed = (P(None, "gx", "gy"), P(None, None, "gx", "gy"))
    return jax.shard_map(
        on_device,
        mesh=mesh,
        in_specs=placed,
        out_specs=(P(None, ("gx", "gy"), None), P(None, None, "gx", "gy")),
        check_vma=False,
    )
```

profile of v0, /device:TPU:0, one launch (start us, length us, event | category | flops | bytes accessed | tf_op | source)
XLA Modules:
  0.0 82.6 jit_solution(3548663355585393147)
XLA Ops:
  0.6 2.9 %fill.1 = (f32[24,8,8,1152]{3,2,1,0:T(8,128)S(1)}, f32[24,8,1152]{2,1,0:T(8,128)S(1)}, f32[155,8,128]{2,1,0:T(8,128)S(1)}, f32[147,8,128]{2,1,0:T(8,128)S(1)}, f...) custom-call(s32[1]{0:T(128)} %bitcast.row_ref._, ...), custom_call_target="tpu_custom_call" | custom-call | tf_op jit(solution)/shard_map/fill/pallas_call | solution.py:575
  3.6 0.0 copy-start.5
  3.6 0.7 copy-done.5
  4.3 0.0 copy-start.4
  4.3 0.5 collective-permute-start.1
  4.8 4.0 %collective-permute-start.2 = (f32[5,8,128]{2,1,0:T(8,128)S(1)}, f32[5,8,128]{2,1,0:T(8,128)S(1)}, u32[]{:S(2)}, u32[]{:S(2)}) collective-permute-start(f32[5,8,128]{2,1,0:T(8,128)S(1)} %get-tuple-element.41), channel_id=1, source_target_pairs={{0,7},{1,0},{2,1},{3,2},{4,3},{5,4},{6,5},{7,6},{8,15},{9,8},{10,9... | collective-permute-start | bytes 61448 | tf_op jit(solution)/shard_map/ppermute | solution.py:544
  8.8 1.5 %collective-permute-done.1.before_ref = f32[5,8,128]{2,1,0:T(8,128)S(1)} collective-permute-done((f32[5,8,128]{2,1,0:T(8,128)S(1)}, f32[5,8,128]{2,1,0:T(8,128)S(1)}, u32[]{:S(2)}, u32[]{:S(2)}) %collective-permute-start.1) | collective-permute-done | bytes 20512 | tf_op jit(solution)/shard_map/ppermute | solution.py:544
  10.2 0.0 collective-permute-done.2.after_ref
  10.3 0.5 side.1
  10.8 0.0 copy-start
  10.8 2.9 %copy-done = f32[24,8,8,1152]{3,2,1,0:T(8,128)} copy-done((f32[24,8,8,1152]{3,2,1,0:T(8,128)}, f32[24,8,8,1152]{3,2,1,0:T(8,128)S(1)}, u32[]{:S(2)}) %copy-start) | copy-done | bytes 7077912
  13.6 2.0 %collective-permute-start.5 = (f32[155,8,128]{2,1,0:T(8,128)S(1)}, f32[155,8,128]{2,1,0:T(8,128)S(1)}, u32[]{:S(2)}, u32[]{:S(2)}) collective-permute-start(f32[155,8,128]{2,1,0:T(8,128)S(1)} %get-tuple-element.47), channel_id=1, source_target_pairs={{0,8},{8,16},{16,24},{24,0},{1,9},{9,17},{17,25},{25,1},{2,10},{10... | collective-permute-start | bytes 1904648 | tf_op jit(solution)/shard_map/ppermute | solution.py:544
  15.6 0.0 copy-done.4
  15.6 1.0 %collective-permute-start.3 = (f32[147,8,128]{2,1,0:T(8,128)S(1)}, f32[147,8,128]{2,1,0:T(8,128)S(1)}, u32[]{:S(2)}, u32[]{:S(2)}) collective-permute-start(f32[147,8,128]{2,1,0:T(8,128)S(1)} %get-tuple-element.46), channel_id=1, source_target_pairs={{0,24},{8,0},{16,8},{24,16},{1,25},{9,1},{17,9},{25,17},{2,26},{10... | collective-permute-start | bytes 1806344 | tf_op jit(solution)/shard_map/ppermute | solution.py:544
  16.6 1.6 %first.1 = f32[128,8,128]{2,1,0:T(8,128)S(1)} custom-call(s32[1]{0:T(128)} %bitcast.row_ref._, s32[1]{0:T(128)} %bitcast.7.__, s32[8,8,128,128]{3,2,1,0:T(8,128)} %bitcast.19), custom_call_target="tpu_custom_call" | custom-call | tf_op jit(solution)/shard_map/first/pallas_call | solution.py:567
  18.2 1.1 %collective-permute-start.4 = (f32[128,8,128]{2,1,0:T(8,128)S(1)}, f32[128,8,128]{2,1,0:T(8,128)S(1)}, u32[]{:S(2)}, u32[]{:S(2)}) collective-permute-start(f32[128,8,128]{2,1,0:T(8,128)S(1)} %first.1), channel_id=1, source_target_pairs={{0,8},{8,16},{16,24},{24,0},{1,9},{9,17},{17,25},{25,1},{2,10},{10... | collective-permute-start | bytes 1572872 | tf_op jit(solution)/shard_map/ppermute | solution.py:544
  19.3 1.9 %collective-permute-start = (f32[64,8,128]{2,1,0:T(8,128)}, f32[64,8,128]{2,1,0:T(8,128)S(1)}, u32[]{:S(2)}, u32[]{:S(2)}) collective-permute-start(f32[64,8,128]{2,1,0:T(8,128)} %copy-done.5), channel_id=1, source_target_pairs={{0,24},{8,0},{16,8},{24,16},{1,25},{9,1},{17,9},{25,17},{2,26},{10... | collective-permute-start | bytes 786440 | tf_op jit(solution)/shard_map/ppermute | solution.py:544
  21.2 1.1 %collective-permute-start.12 = (f32[72,8,128]{2,1,0:T(8,128)}, f32[72,8,128]{2,1,0:T(8,128)S(1)}, u32[]{:S(2)}, u32[]{:S(2)}) collective-permute-start(f32[72,8,128]{2,1,0:T(8,128)} %copy-done.4), channel_id=1, source_target_pairs={{0,24},{8,0},{16,8},{24,16},{1,25},{9,1},{17,9},{25,17},{2,26},{10... | collective-permute-start | bytes 884744 | tf_op jit(solution)/shard_map/ppermute | solution.py:544
  22.3 0.0 copy-start.1
  22.3 3.0 %copy-done.1 = f32[24,8,8,1152]{3,2,1,0:T(8,128)S(1)} copy-done((f32[24,8,8,1152]{3,2,1,0:T(8,128)S(1)}, f32[24,8,8,1152]{3,2,1,0:T(8,128)}, u32[]{:S(2)}) %copy-start.1) | copy-done | bytes 7077912
  25.3 0.0 copy-start.2
  25.3 13.0 %interior.1 = (f32[22,8,8,1152]{3,2,1,0:T(8,128)S(1)}, f32[20,8,8,1152]{3,2,1,0:T(8,128)S(1)}, f32[18,8,8,1152]{3,2,1,0:T(8,128)S(1)}, f32[16,8,8,1024]{3,2,1,0:T(8,128)S(1)}, f32[24,128]{1,0:T(8,128)S(1)}) custom-call(f32[24,8,8,1152]{3,2,1,0:T(8,128)S(1)} %copy-done.1, f32[24,8,1152]{2,1,0:T(8,128)S(1)} %get-tuple-element.49.ons.refs_7_), custom_call_target="tpu_custom_call" | custom-call | tf_op jit(solution)/shard_map/interior/pallas_call | solution.py:600
  38.4 17.5 %collective-permute-done.4.refs_0_ = f32[128,8,128]{2,1,0:T(8,128)S(1)} collective-permute-done((f32[128,8,128]{2,1,0:T(8,128)S(1)}, f32[128,8,128]{2,1,0:T(8,128)S(1)}, u32[]{:S(2)}, u32[]{:S(2)}) %collective-permute-start.4) | collective-permute-done | bytes 524320 | tf_op jit(solution)/shard_map/ppermute | solution.py:544
  55.9 0.0 collective-permute-done.5.refs_1_
  55.9 0.0 copy-done.2
  55.9 4.9 %shard_map.50 = (f32[24,8,8,1152]{3,2,1,0:T(8,128)S(1)}, f32[22,8,8,1152]{3,2,1,0:T(8,128)S(1)}, f32[20,8,8,1152]{3,2,1,0:T(8,128)S(1)}, f32[18,8,8,1152]{3,2,1,...) custom-call(f32[128,8,128]{2,1,0:T(8,128)S(1)} %collective-permute-d, ...), custom_call_target="tpu_custom_call", output_to_operand_aliasing={{0}: (2, {}), {1}: (3, {}), {2}: (4, {}), {3}: (5, {}), {4}... | custom-call | tf_op jit(solution)/shard_map/pallas_call | solution.py:609
  60.8 0.0 collective-permute-done.3.refs_0_
  60.8 3.0 %shard_map.51 = (f32[24,8,8,1152]{3,2,1,0:T(8,128)S(1)}, f32[22,8,8,1152]{3,2,1,0:T(8,128)S(1)}, f32[20,8,8,1152]{3,2,1,0:T(8,128)S(1)}, f32[18,8,8,1152]{3,2,1,...) custom-call(f32[147,8,128]{2,1,0:T(8,128)S(1)} %collective-permute-d, ...), custom_call_target="tpu_custom_call", output_to_operand_aliasing={{0}: (1, {}), {1}: (2, {}), {2}: (3, {}), {3}: (4, {}), {4}... | custom-call | tf_op jit(solution)/shard_map/pallas_call | solution.py:609
  63.8 0.0 collective-permute-done.refs_0_
  63.8 0.0 copy-start.6
  63.8 0.0 copy-start.3
  63.8 1.6 %shard_map.52 = (f32[24,8,8,1152]{3,2,1,0:T(8,128)S(1)}, f32[22,8,8,1152]{3,2,1,0:T(8,128)S(1)}, f32[20,8,8,1152]{3,2,1,0:T(8,128)S(1)}, f32[18,8,8,1152]{3,2,1,...) custom-call(f32[64,8,128]{2,1,0:T(8,128)S(1)} %collective-permute-do, ...), custom_call_target="tpu_custom_call", output_to_operand_aliasing={{0}: (1, {}), {1}: (2, {}), {2}: (3, {}), {3}: (4, {}), {4}... | custom-call | tf_op jit(solution)/shard_map/pallas_call | solution.py:609
  65.5 0.0 collective-permute-start.6
  65.5 0.1 sqrt_atan2_fusion
  65.6 1.0 %collective-permute-done.6 = f32[8,128]{1,0:T(8,128)S(1)} collective-permute-done((f32[8,128]{1,0:T(8,128)S(1)}, f32[8,128]{1,0:T(8,128)S(1)}, u32[]{:S(2)}, u32[]{:S(2)}) %collective-permute-start.6) | collective-permute-done | bytes 4128 | tf_op jit(solution)/shard_map/ppermute | solution.py:528
  66.7 0.4 collective-permute-start.7
  67.1 3.2 %collective-permute-done.7 = f32[8,128]{1,0:T(8,128)S(1)} collective-permute-done((f32[8,128]{1,0:T(8,128)S(1)}, f32[8,128]{1,0:T(8,128)S(1)}, u32[]{:S(2)}, u32[]{:S(2)}) %collective-permute-start.7) | collective-permute-done | bytes 4128 | tf_op jit(solution)/shard_map/ppermute | solution.py:528
  70.3 1.4 %collective-permute-start.8 = (f32[8,128]{1,0:T(8,128)S(1)}, f32[8,128]{1,0:T(8,128)S(1)}, u32[]{:S(2)}, u32[]{:S(2)}) collective-permute-start(f32[8,128]{1,0:T(8,128)S(1)} %add.55), channel_id=1, source_target_pairs={{0,4},{1,5},{2,6},{3,7},{4,0},{5,1},{6,2},{7,3},{8,12},{9,13},{10,... | collective-permute-start | bytes 12296 | tf_op jit(solution)/shard_map/ppermute | solution.py:528
  71.7 0.0 copy-done.6
  71.7 0.1 fusion.1
  71.8 2.9 %collective-permute-done.8 = f32[8,128]{1,0:T(8,128)S(1)} collective-permute-done((f32[8,128]{1,0:T(8,128)S(1)}, f32[8,128]{1,0:T(8,128)S(1)}, u32[]{:S(2)}, u32[]{:S(2)}) %collective-permute-start.8) | collective-permute-done | bytes 4128 | tf_op jit(solution)/shard_map/ppermute | solution.py:528
  74.8 2.0 %collective-permute-start.10 = (f32[8,128]{1,0:T(8,128)S(1)}, f32[8,128]{1,0:T(8,128)S(1)}, u32[]{:S(2)}, u32[]{:S(2)}) collective-permute-start(f32[8,128]{1,0:T(8,128)S(1)} %add.56), channel_id=1, source_target_pairs={{0,16},{8,24},{16,0},{24,8},{1,17},{9,25},{17,1},{25,9},{2,18},{10... | collective-permute-start | bytes 12296 | tf_op jit(solution)/shard_map/ppermute | solution.py:524
  76.8 0.5 collective-permute-start.11
  77.3 1.0 %collective-permute-start.9 = (f32[8,128]{1,0:T(8,128)S(1)}, f32[8,128]{1,0:T(8,128)S(1)}, u32[]{:S(2)}, u32[]{:S(2)}) collective-permute-start(f32[8,128]{1,0:T(8,128)S(1)} %add.56), channel_id=1, source_target_pairs={{0,8},{8,0},{16,24},{24,16},{1,9},{9,1},{17,25},{25,17},{2,10},{10... | collective-permute-start | bytes 12296 | tf_op jit(solution)/shard_map/ppermute | solution.py:524
  78.3 0.0 collective-permute-done.12.dc_ref
  78.3 0.0 copy-done.3
  78.3 2.5 %last.1 = f32[8,8,128,128]{3,2,1,0:T(8,128)} custom-call(f32[72,8,128]{2,1,0:T(8,128)S(1)} %collective-permute-done.12.dc_ref, f32[6,8,8,1152]{3,2,1,0:T(8,128)S(1)} %get-tuple-element.71.edge_ref, f32[2,8,1152]{2,1,0:T(8,128)S(1)} %get-tuple-element.72.eons_ref, f32[2,8,8,1024]{3,2,1,0:T(8,128)S(1)} %get-tuple-element.73.tail_ref, ...), custom_call_target="tpu_custom_call", output_to_operand_aliasing={{}: (5, {})} | custom-call | tf_op jit(solution)/shard_map/last/pallas_call | solution.py:635
  80.8 0.0 collective-permute-done.10
  80.8 0.5 collective-permute-done.11
  81.3 0.0 collective-permute-done.9
  81.3 1.3 %green.1 = f32[2,64,256]{2,1,0:T(8,128)} custom-call(f32[8,512]{1,0:T(8,128)S(1)} %pad_maximum_fusion.tables_ref, f32[8,128]{1,0:T(8,128)S(1)} %add_add_fusion.packed_ref), custom_call_target="tpu_custom_call" | custom-call | tf_op jit(solution)/shard_map/green/pallas_call | solution.py:652
  (6 shorter events, 0.0 us)
Async XLA Ops:
  3.6 0.7 copy-start.5
  4.3 11.4 %copy-start.4 = (f32[72,8,128]{2,1,0:T(8,128)}, f32[72,8,128]{2,1,0:T(8,128)S(1)}, u32[]{:S(2)}) copy-start(f32[72,8,128]{2,1,0:T(8,128)S(1)} %get-tuple-element.70) | copy-start | bytes 884740
  4.3 6.0 %collective-permute-start.1 = (f32[5,8,128]{2,1,0:T(8,128)S(1)}, f32[5,8,128]{2,1,0:T(8,128)S(1)}, u32[]{:S(2)}, u32[]{:S(2)}) collective-permute-start(f32[5,8,128]{2,1,0:T(8,128)S(1)} %get-tuple-element.40), channel_id=1, source_target_pairs={{0,1},{1,2},{2,3},{3,4},{4,5},{5,6},{6,7},{7,0},{8,9},{9,10},{10,1... | collective-permute-start | bytes 61448 | tf_op jit(solution)/shard_map/ppermute | solution.py:544
  4.8 5.5 %collective-permute-start.2 = (f32[5,8,128]{2,1,0:T(8,128)S(1)}, f32[5,8,128]{2,1,0:T(8,128)S(1)}, u32[]{:S(2)}, u32[]{:S(2)}) collective-permute-start(f32[5,8,128]{2,1,0:T(8,128)S(1)} %get-tuple-element.41), channel_id=1, source_target_pairs={{0,7},{1,0},{2,1},{3,2},{4,3},{5,4},{6,5},{7,6},{8,15},{9,8},{10,9... | collective-permute-start | bytes 61448 | tf_op jit(solution)/shard_map/ppermute | solution.py:544
  10.8 2.9 %copy-start = (f32[24,8,8,1152]{3,2,1,0:T(8,128)}, f32[24,8,8,1152]{3,2,1,0:T(8,128)S(1)}, u32[]{:S(2)}) copy-start(f32[24,8,8,1152]{3,2,1,0:T(8,128)S(1)} %get-tuple-element.48.v_ref.refs_2_) | copy-start | bytes 21233668
  13.6 42.2 %collective-permute-start.5 = (f32[155,8,128]{2,1,0:T(8,128)S(1)}, f32[155,8,128]{2,1,0:T(8,128)S(1)}, u32[]{:S(2)}, u32[]{:S(2)}) collective-permute-start(f32[155,8,128]{2,1,0:T(8,128)S(1)} %get-tuple-element.47), channel_id=1, source_target_pairs={{0,8},{8,16},{16,24},{24,0},{1,9},{9,17},{17,25},{25,1},{2,10},{10... | collective-permute-start | bytes 1904648 | tf_op jit(solution)/shard_map/ppermute | solution.py:544
  15.6 45.1 %collective-permute-start.3 = (f32[147,8,128]{2,1,0:T(8,128)S(1)}, f32[147,8,128]{2,1,0:T(8,128)S(1)}, u32[]{:S(2)}, u32[]{:S(2)}) collective-permute-start(f32[147,8,128]{2,1,0:T(8,128)S(1)} %get-tuple-element.46), channel_id=1, source_target_pairs={{0,24},{8,0},{16,8},{24,16},{1,25},{9,1},{17,9},{25,17},{2,26},{10... | collective-permute-start | bytes 1806344 | tf_op jit(solution)/shard_map/ppermute | solution.py:544
  18.2 37.6 %collective-permute-start.4 = (f32[128,8,128]{2,1,0:T(8,128)S(1)}, f32[128,8,128]{2,1,0:T(8,128)S(1)}, u32[]{:S(2)}, u32[]{:S(2)}) collective-permute-start(f32[128,8,128]{2,1,0:T(8,128)S(1)} %first.1), channel_id=1, source_target_pairs={{0,8},{8,16},{16,24},{24,0},{1,9},{9,17},{17,25},{25,1},{2,10},{10... | collective-permute-start | bytes 1572872 | tf_op jit(solution)/shard_map/ppermute | solution.py:544
  19.3 44.5 %collective-permute-start = (f32[64,8,128]{2,1,0:T(8,128)}, f32[64,8,128]{2,1,0:T(8,128)S(1)}, u32[]{:S(2)}, u32[]{:S(2)}) collective-permute-start(f32[64,8,128]{2,1,0:T(8,128)} %copy-done.5), channel_id=1, source_target_pairs={{0,24},{8,0},{16,8},{24,16},{1,25},{9,1},{17,9},{25,17},{2,26},{10... | collective-permute-start | bytes 786440 | tf_op jit(solution)/shard_map/ppermute | solution.py:544
  21.2 57.1 %collective-permute-start.12 = (f32[72,8,128]{2,1,0:T(8,128)}, f32[72,8,128]{2,1,0:T(8,128)S(1)}, u32[]{:S(2)}, u32[]{:S(2)}) collective-permute-start(f32[72,8,128]{2,1,0:T(8,128)} %copy-done.4), channel_id=1, source_target_pairs={{0,24},{8,0},{16,8},{24,16},{1,25},{9,1},{17,9},{25,17},{2,26},{10... | collective-permute-start | bytes 884744 | tf_op jit(solution)/shard_map/ppermute | solution.py:544
  22.3 3.0 %copy-start.1 = (f32[24,8,8,1152]{3,2,1,0:T(8,128)S(1)}, f32[24,8,8,1152]{3,2,1,0:T(8,128)}, u32[]{:S(2)}) copy-start(f32[24,8,8,1152]{3,2,1,0:T(8,128)} %copy-done) | copy-start | bytes 21233668
  25.3 30.5 %copy-start.2 = (f32[24,8,8,1152]{3,2,1,0:T(8,128)S(1)}, f32[24,8,8,1152]{3,2,1,0:T(8,128)}, u32[]{:S(2)}) copy-start(f32[24,8,8,1152]{3,2,1,0:T(8,128)} %copy-done) | copy-start | bytes 21233668
  63.8 7.9 %copy-start.6 = (f32[8]{0:T(128)S(1)}, f32[8]{0:T(128)}, u32[]{:S(2)}) copy-start(f32[8]{0:T(128)} %constant.29) | copy-start | bytes 100
  63.8 14.4 %copy-start.3 = (f32[8,8,8,1024]{3,2,1,0:T(8,128)S(1)}, f32[8,8,8,1024]{3,2,1,0:T(8,128)}, u32[]{:S(2)}) copy-start(f32[8,8,8,1024]{3,2,1,0:T(8,128)} %get-tuple-element.74.top_ref) | copy-start | bytes 6291460
  65.5 1.2 %collective-permute-start.6 = (f32[8,128]{1,0:T(8,128)S(1)}, f32[8,128]{1,0:T(8,128)S(1)}, u32[]{:S(2)}, u32[]{:S(2)}) collective-permute-start(f32[8,128]{1,0:T(8,128)S(1)} %get-tuple-element.69), channel_id=1, source_target_pairs={{0,1},{1,0},{2,3},{3,2},{4,5},{5,4},{6,7},{7,6},{8,9},{9,8},{10,11... | collective-permute-start | bytes 12296 | tf_op jit(solution)/shard_map/ppermute | solution.py:528
  66.7 3.6 %collective-permute-start.7 = (f32[8,128]{1,0:T(8,128)S(1)}, f32[8,128]{1,0:T(8,128)S(1)}, u32[]{:S(2)}, u32[]{:S(2)}) collective-permute-start(f32[8,128]{1,0:T(8,128)S(1)} %add.54), channel_id=1, source_target_pairs={{0,2},{1,3},{2,0},{3,1},{4,6},{5,7},{6,4},{7,5},{8,10},{9,11},{10,... | collective-permute-start | bytes 12296 | tf_op jit(solution)/shard_map/ppermute | solution.py:528
  70.3 4.5 %collective-permute-start.8 = (f32[8,128]{1,0:T(8,128)S(1)}, f32[8,128]{1,0:T(8,128)S(1)}, u32[]{:S(2)}, u32[]{:S(2)}) collective-permute-start(f32[8,128]{1,0:T(8,128)S(1)} %add.55), channel_id=1, source_target_pairs={{0,4},{1,5},{2,6},{3,7},{4,0},{5,1},{6,2},{7,3},{8,12},{9,13},{10,... | collective-permute-start | bytes 12296 | tf_op jit(solution)/shard_map/ppermute | solution.py:528
  74.8 6.0 %collective-permute-start.10 = (f32[8,128]{1,0:T(8,128)S(1)}, f32[8,128]{1,0:T(8,128)S(1)}, u32[]{:S(2)}, u32[]{:S(2)}) collective-permute-start(f32[8,128]{1,0:T(8,128)S(1)} %add.56), channel_id=1, source_target_pairs={{0,16},{8,24},{16,0},{24,8},{1,17},{9,25},{17,1},{25,9},{2,18},{10... | collective-permute-start | bytes 12296 | tf_op jit(solution)/shard_map/ppermute | solution.py:524
  76.8 4.5 %collective-permute-start.11 = (f32[8,128]{1,0:T(8,128)S(1)}, f32[8,128]{1,0:T(8,128)S(1)}, u32[]{:S(2)}, u32[]{:S(2)}) collective-permute-start(f32[8,128]{1,0:T(8,128)S(1)} %add.56), channel_id=1, source_target_pairs={{0,24},{8,16},{16,8},{24,0},{1,25},{9,17},{17,9},{25,1},{2,26},{10... | collective-permute-start | bytes 12296 | tf_op jit(solution)/shard_map/ppermute | solution.py:524
  77.3 4.0 %collective-permute-start.9 = (f32[8,128]{1,0:T(8,128)S(1)}, f32[8,128]{1,0:T(8,128)S(1)}, u32[]{:S(2)}, u32[]{:S(2)}) collective-permute-start(f32[8,128]{1,0:T(8,128)S(1)} %add.56), channel_id=1, source_target_pairs={{0,8},{8,0},{16,24},{24,16},{1,9},{9,1},{17,25},{25,17},{2,10},{10... | collective-permute-start | bytes 12296 | tf_op jit(solution)/shard_map/ppermute | solution.py:524
where the time goes:
time: 82.8 us; the launch traced here: 82.6 us
  Pallas kernels  31.5 us (38%)
  waiting for transfers between devices  26.6 us (32%)
  starting transfers between devices  16.9 us (20%)
  local copies, waits for them, and re-layouts  6.58 us (8%)
    ppermute x7, waiting for transfers between devices, send(): lax.ppermute(array, axis, [(i, (i + step) % peers) for i in range(peers)])  19 us
    pallas_call x1, Pallas kernels, on_device(): pl.pallas_call(functools.partial(interior_kernel, d), out_shape=vectors[1...  13 us
    ppermute x7, starting transfers between devices, send(): lax.ppermute(array, axis, [(i, (i + step) % peers) for i in range(peers)])  11.6 us
    pallas_call x3, Pallas kernels, wave(): pl.pallas_call(functools.partial(wave_kernel, d, names, waves), out_shape...  9.56 us
    ppermute x3, waiting for transfers between devices, add_over(): lax.ppermute(value, axis, [(i, i ^ shift) for i in range(peers)])  7.14 us
    unnamed x14, local copies, waits for them, and re-layouts  6.58 us
    ppermute x3, starting transfers between devices, add_over(): lax.ppermute(value, axis, [(i, i ^ s) for i in range(peers)])  3.49 us
    pallas_call x1, Pallas kernels, on_device(): pl.pallas_call(functools.partial(fill_kernel, d), out_shape=[vectors[0],...  2.92 us
  transfers between devices with their start and end apart: 13, of which 6 were waited for; matrix products, arithmetic and copies ran while one was open for 0% of the time, Pallas kernels for 32%

commit v1 on v0

--- a/solution.py
+++ b/solution.py
@@ -71,21 +71,25 @@
         self.row_tiles = self.pl * self.ct
         self.per_corner = LANES // (2 * STEPS)
         self.per_edge = LANES // STEPS
-        self.corner_v = -(-STEPS * self.pl // self.per_corner)
-        self.corner_tiles = self.corner_v + 1
         self.edge_v = -(-self.rows * self.pl // self.per_edge)
         self.edge_tiles = self.edge_v + -(-self.rows // self.per_edge)
         self.plan = {
-            "ua": ((1, 2), (), False),
-            "ub": ((3, 4), (1, 2, 3), True),
-            "da": ((1, 2), (1, 2), True),
-            "db": ((3,), (), False),
-            "dc": ((4,), (3,), False),
+            "ua": (((0, 1), (0, 2)), 0, ()),
+            "ub": (((1, 2), (2, 2)), 1, ((0, 1), (0, 2), (1, 2))),
+            "da": (((0, 1), (0, 2)), 1, ((0, 1), (0, 2))),
+            "db": (((1, 2),), 0, ((1, 2),)),
+            "dc": (((2, 2),), 0, ()),
         }
 
+    def places(self, name):
+        rows, onsite, corners = self.plan[name]
+        first = len(rows) * self.row_tiles
+        second = first + onsite * self.ct
+        third = second - (-len(corners) * self.pl // self.per_corner)
+        return first, second, third, third + (onsite if corners else 0)
+
     def tiles(self, name):
-        v_rows, o_rows, corners = self.plan[name]
-        return len(v_rows) * self.row_tiles + len(o_rows) * self.ct + corners * self.corner_tiles
+        return self.places(name)[-1]
 
     def halo(self, name, k):
         return STEPS - k if name[0] == "u" else STEPS + self.rows - 1 + k
@@ -102,7 +106,7 @@
     return (2 * bits - 1).astype(F32)
 
 
-def first_kernel(d, _, __, bits_ref, out_ref, scratch, sem):
+def first_kernel(d, __, ___, bits_ref, out_ref, scratch, sem):
     size = d.ct * SUB
     copies = [
         pltpu.make_async_copy(
@@ -115,15 +119,15 @@
     for p, copy in enumerate(copies):
         copy.wait()
         flat = scratch.at[p].reshape(d.q * size, LANES)
-        for i, k in enumerate(d.plan["ua"][0]):
+        for i, (_, k) in enumerate(d.plan["ua"][0]):
             for t in range(d.ct):
                 bits = flat[pl.ds(t * SUB + SUB - k, d.q, stride=size), :]
                 out_ref[i * d.row_tiles + p * d.ct + t] = to_spin(bits)
 
 
-def fill_kernel(d, row_ref, bits_ref, levels_ref, v_ref, ons_ref, *refs):
-    sends = dict(zip(("ub", "da", "db", "dc"), refs))
-    right_ref, left_ref, scratch, lscratch, sem = refs[4:]
+def fill_kernel(
+    d, row_ref, bits_ref, levels_ref, v_ref, ons_ref, da_ref, right_ref, left_ref, scratch, lscratch, sem
+):
     lcopy = pltpu.make_async_copy(levels_ref, lscratch, sem.at[d.pl])
     copies = [
         pltpu.make_async_copy(bits_ref.at[:, p], scratch.at[p], sem.at[p]) for p in range(d.pl)
@@ -174,19 +178,24 @@
         pack(spins, ref, 0, low_side)
         onsite = [lambda r=r: ons_ref[STEPS + r, :, at] for r in range(d.rows)]
         pack(onsite, ref, d.edge_v, low_side)
-    for name, ref in sends.items():
-        v_rows, o_rows, _ = d.plan[name]
-        for i, k in enumerate(v_rows):
+    put_rows(d, "da", da_ref, {0: Rows(v_ref, 0)}, ons_ref)
+
+
+def put_rows(d, name, ref, v, ons_ref):
+    rows, onsite, _ = d.plan[name]
+    for i, (n, k) in enumerate(rows):
+        if n in v:
             for p in range(d.pl):
                 for t in range(d.ct):
-                    ref[i * d.row_tiles + p * d.ct + t] = v_ref[d.source(name, k), p, :, lanes_of(t)]
-        base = len(v_rows) * d.row_tiles
-        for i, k in enumerate(o_rows):
-            for t in range(d.ct):
-                ref[base + i * d.ct + t] = ons_ref[d.source(name, k), :, lanes_of(t)]
-
-
-def side_kernel(d, before_ref, after_ref, v_in, o_in, ub_in, da_in, v_ref, ons_ref, ub_ref, da_ref):
+                    ref[i * d.row_tiles + p * d.ct + t] = v[n][d.source(name, k), p, :, lanes_of(t)]
+    if onsite:
+        for t in range(d.ct):
+            ref[d.places(name)[0] + t] = ons_ref[d.source(name, 1), :, lanes_of(t)]
+
+
+def side_kernel(
+    d, before_ref, after_ref, v_in, o_in, da_in, v_ref, ons_ref, da_ref, ub_ref, db_ref, dc_ref, work
+):
     lane = lax.broadcasted_iota(jnp.int32, (SUB, LANES), 1)
     low, high = lane < STEPS, lane >= LANES - STEPS
 
@@ -201,58 +210,71 @@
         for p in range(d.pl):
             v_ref[STEPS + r, p, :, at] = side(0, r * d.pl + p)
         ons_ref[STEPS + r, :, at] = side(d.edge_v, r)
-    for name, ref in (("ub", ub_ref), ("da", da_ref)):
-        spins = [
-            v_ref[d.source(name, k), p, :, at] for k in range(1, STEPS + 1) for p in range(d.pl)
-        ]
-        onsite = [ons_ref[d.source(name, k), :, at] for k in range(1, STEPS)]
-        base = d.tiles(name) - d.corner_tiles
-        for items, first in ((spins, base), (onsite, base + d.corner_v)):
-            for start in range(0, len(items), d.per_corner):
-                total = None
-                for g, item in enumerate(items[start : start + d.per_corner]):
-                    moved = pltpu.roll(item, (STEPS + 2 * STEPS * g) % LANES, 1)
-                    total = moved if total is None else total + moved
-                ref[first + start // d.per_corner] = total
-
-
-def install(d, name, ref, v_ref, ons_ref):
-    v_rows, o_rows, corners = d.plan[name]
-    for i, k in enumerate(v_rows):
+    v0 = Rows(v_ref, 0)
+    for letter, named in (("u", {"ub": ub_ref}), ("d", {"da": da_ref, "db": db_ref, "dc": dc_ref})):
+        second, third = d.source(letter, 2), d.source(letter, 3)
+        v = (v0, Rows(work, -min(second, third)))
+        for row in (third, second):
+            one_row(d, 1, row, v, ons_ref)
+        part = Rows(work, 2 - second)
+        for p, value in enumerate(row_values(d, 2, second, v, ons_ref, leave=2 * second - third)):
+            part[second, p] = value
+        v = {0: v0, 1: v[1], 2: part}
+        for name, ref in named.items():
+            if name != "da":
+                put_rows(d, name, ref, v, ons_ref)
+            _, onsite, corners = d.plan[name]
+            _, start, onsite_at, _ = d.places(name)
+            packs = [(start, [(v[n], d.source(name, k), p) for n, k in corners for p in range(d.pl)])]
+            for start, items in packs:
+                for base in range(0, len(items), d.per_corner):
+                    total = None
+                    for g, (rows, row, p) in enumerate(items[base : base + d.per_corner]):
+                        tile = jnp.where(low | high, rows[row, p, :, at], 0.0)
+                        moved = pltpu.roll(tile, (STEPS + 2 * STEPS * g) % LANES, 1)
+                        total = moved if total is None else total + moved
+                    ref[start + base // d.per_corner] = total
+            if onsite:
+                ref[onsite_at] = ons_ref[d.source(name, 1), :, at]
+
+
+def install(d, name, ref, v, ons_ref):
+    rows, onsite, corners = d.plan[name]
+    first, second, third, _ = d.places(name)
+    for i, (n, k) in enumerate(rows):
         for p in range(d.pl):
             for t in range(d.ct):
-                v_ref[d.halo(name, k), p, :, lanes_of(t)] = ref[i * d.row_tiles + p * d.ct + t]
-    base = len(v_rows) * d.row_tiles
-    for i, k in enumerate(o_rows):
+                v[n][d.halo(name, k), p, :, lanes_of(t)] = ref[i * d.row_tiles + p * d.ct + t]
+            if n == 2:
+                v[n][d.halo(name, k), p, :, d.cols :] = jnp.zeros((d.q, LANES), F32)
+    at = slice(d.cols, d.width)
+    if onsite:
         for t in range(d.ct):
-            ons_ref[d.halo(name, k), :, lanes_of(t)] = ref[base + i * d.ct + t]
-    if not corners:
-        return
+            ons_ref[d.halo(name, 1), :, lanes_of(t)] = ref[first + t]
+        ons_ref[d.halo(name, 1), :, at] = ref[third]
     lane = lax.broadcasted_iota(jnp.int32, (SUB, LANES), 1)
     edge = (lane < STEPS) | (lane >= LANES - STEPS)
-    at = slice(d.cols, d.width)
-
-    def corner(first, i):
-        tile, g = first + i // d.per_corner, i % d.per_corner
-        moved = pltpu.roll(ref[tile], (-(STEPS + 2 * STEPS * g)) % LANES, 1)
-        return jnp.where(edge, moved, 0.0)
-
-    base = d.tiles(name) - d.corner_tiles
-    for k in range(1, STEPS + 1):
+    for i, (n, k) in enumerate(corners):
         for p in range(d.pl):
-            v_ref[d.halo(name, k), p, :, at] = corner(base, (k - 1) * d.pl + p)
-        if k < STEPS:
-            ons_ref[d.halo(name, k), :, at] = corner(base + d.corner_v, k - 1)
-
-
-def row_values(d, n, at, v, ons, one_sided=False):
+            j = i * d.pl + p
+            tile, g = second + j // d.per_corner, j % d.per_corner
+            moved = pltpu.roll(ref[tile], (-(STEPS + 2 * STEPS * g)) % LANES, 1)
+            v[n][d.halo(name, k), p, :, at] = jnp.where(edge, moved, 0.0)
+
+
+def complete(d, letter, v):
+    for p in range(d.pl):
+        far, near = d.halo(letter, 2), d.halo(letter, 1)
+        v[2][far, p] = v[2][far, p] - HOP * v[1][near, p]
+
+
+def row_values(d, n, at, v, ons, leave=None):
     source = v[n - 1]
     values = []
     for p in range(d.pl):
         x = source[at, p]
-        beside = source[at - 1, p]
-        if not one_sided:
-            beside = beside + source[at + 1, p]
+        near = [source[row, p] for row in (at + 1, at - 1) if row != leave]
+        beside = near[0] if leave is not None else near[0] + near[1]
         beside = beside + pltpu.roll(x, 1, 1) + pltpu.roll(x, d.width - 1, 1)
         if p + 1 < d.pl:
             beside = beside + source[at, p + 1]
@@ -268,7 +290,7 @@
         if n < STEPS:
             v[n][at, p] = value
         else:
-            v[n][at - STEPS, p, :, : d.cols] = value[:, : d.cols]
+            v[n][at - STEPS, p] = value[:, : d.cols]
 
 
 def split_pair(x):
@@ -322,15 +344,10 @@
             at = row + STEPS
             one_row(d, n, at, v, ons)
             if n == STEPS:
-                add_gram(gram_ref, gram_row(d, at, v, lambda p: v[n][row, p, :, : d.cols]))
+                add_gram(gram_ref, gram_row(d, at, v, lambda p: v[n][row, p]))
             return 0
 
         lax.fori_loop(n, d.rows - n, step, 0)
-
-
-def edge_rows(d):
-    top = STEPS + d.rows - 1
-    return [(n, top + STEPS - 1 - n - i) for n in range(STEPS - 1) for i in range(2)]
 
 
 def wave_kernel(d, names, waves, *refs):
@@ -339,48 +356,35 @@
     v = all_rows(refs[: STEPS + 1])
     ons, gram_ref, *extra = refs[STEPS + 1 :]
     for name, ref in zip(names, recv):
-        install(d, name, ref, v[0], ons)
+        install(d, name, ref, v, ons)
 
     def gram(at, last=None):
-        part = gram_row(d, at, v, last or (lambda p: v[STEPS][at - STEPS, p, :, : d.cols]))
+        part = gram_row(d, at, v, last or (lambda p: v[STEPS][at - STEPS, p]))
         add_gram(gram_ref, part)
 
+    top = STEPS + d.rows - 1
     for side, k in waves:
-        at_of = lambda n: STEPS + n - k if side == "u" else STEPS + d.rows - 1 - (n - k)
-        for n in range(1, STEPS):
+        at_of = lambda n: STEPS + n - k if side == "u" else top - (n - k)
+        if k == STEPS:
+            complete(d, side, v)
+        for n in range(max(1, k - 1), STEPS):
             one_row(d, n, at_of(n), v, ons)
         at = at_of(STEPS)
-        if k < STEPS:
+        if side == "u" or k < STEPS - 1:
             one_row(d, STEPS, at, v, ons)
-            gram(at)
-        elif side == "u":
-            one_row(d, STEPS, at, v, ons)
-            gram(at, lambda p: v[STEPS][0, p, :, : d.cols] - HOP * v[STEPS - 1][at - 1, p, :, : d.cols])
-    if ("d", STEPS - 1) in waves:
-        at = STEPS + d.rows - 1
-        for p, value in enumerate(row_values(d, STEPS, at, v, ons, one_sided=True)):
-            v[STEPS][d.rows - 1, p, :, : d.cols] = value[:, : d.cols]
-        gram(at)
+            inner = HOP if side == "u" and k == STEPS else None
+            gram(at, inner and (lambda p: v[STEPS][0, p] - inner * v[STEPS - 1][at - 1, p, :, : d.cols]))
     if ("u", STEPS) in waves:
         flush(d, v[STEPS], *extra)
     if ("d", STEPS - 2) in waves:
-        top_ref, sem = extra
-        done = d.rows - 2 - (d.rt - 1) * SUB
-        copy = pltpu.make_async_copy(
-            v[STEPS].rows((d.rt - 1) * SUB, done).at[:, :, :, pl.ds(0, d.cols)],
-            top_ref.at[pl.ds(0, done)], sem,
-        )
-        copy.start()
-        copy.wait()
+        for p, value in enumerate(row_values(d, STEPS, top - 1, v, ons, leave=top)):
+            v[STEPS][d.rows - 2, p] = value[:, : d.cols]
+        gram(top - 1)
     if ("d", STEPS - 1) in waves:
-        edge_ref, eons_ref, tail_ref, packed_ref = extra
-        for i, (n, at) in enumerate(edge_rows(d)):
-            edge_ref[i] = v[n][at]
-        for k in range(1, STEPS - 1):
-            eons_ref[k - 1] = ons[d.halo("dc", k)]
-        for i in range(2):
-            tail_ref[i] = v[STEPS][d.rows - 2 + i, :, :, : d.cols]
-        packed_ref[...] = packed_gram(d, gram_ref[...])
+        for p, value in enumerate(row_values(d, STEPS, top, v, ons, leave=top + 1)):
+            v[STEPS][d.rows - 1, p] = value[:, : d.cols]
+        gram(top, lambda p: v[STEPS][d.rows - 1, p] - HOP * v[STEPS - 1][top - 1, p, :, : d.cols])
+        extra[0][...] = packed_gram(d, gram_ref[...])
 
 
 def transpose_tiles(d, r, p, rows, stage):
@@ -403,55 +407,42 @@
         copy.wait()
 
 
-def last_kernel(
-    d, dc_ref, edge_ref, eons_ref, tail_ref, top_ref, _, out_ref, work, wons, rows, stage, sem, osem
-):
-    loads = [
-        pltpu.make_async_copy(top_ref.at[pl.ds(0, SUB - 2), p], rows.at[p, pl.ds(0, SUB - 2)], sem.at[p])
-        for p in range(d.pl)
-    ]
-    for load in loads:
-        load.start()
-    for n in range(STEPS - 1):
-        for i in range(2):
-            work[3 * n + 1 + i] = edge_ref[2 * n + i]
-    for i in range(d.row_tiles):
-        p, t = i // d.ct, i % d.ct
-        work[0, p, :, lanes_of(t)] = dc_ref[i]
-    for t in range(d.ct):
-        wons[0, :, lanes_of(t)] = dc_ref[d.row_tiles + t]
-    work[0, :, :, d.cols :] = jnp.zeros((d.pl, d.q, LANES), F32)
-    wons[0, :, d.cols :] = jnp.zeros((d.pl, LANES), F32)
-    for k in range(STEPS - 2):
-        wons[STEPS - 2 - k] = eons_ref[k]
-    for n in range(1, STEPS):
-        base = 3 * (n - 1)
-        for p in range(d.pl):
-            x = work[base + 1, p]
-            beside = work[base, p] + work[base + 2, p]
-            beside = beside + pltpu.roll(x, 1, 1) + pltpu.roll(x, d.width - 1, 1)
-            if p + 1 < d.pl:
-                beside = beside + work[base + 1, p + 1]
-            if p > 0:
-                beside = beside + work[base + 1, p - 1]
-            value = wons[n - 1, pl.ds(p, SUB, stride=0), :] * x - HOP * beside
-            work[3 * n, p] = 0.5 * value if n == 1 else value - work[base - 1, p]
+def last_kernel(d, dc_ref, *refs):
+    out_ref, *refs = refs[STEPS + 3 :]
+    v, (ons, stage, sem) = all_rows(refs[: STEPS + 1]), refs[STEPS + 1 :]
+    install(d, "dc", dc_ref, v, ons)
+    complete(d, "d", v)
+    top = STEPS + d.rows - 1
+    one_row(d, STEPS - 1, top + 1, v, ons)
     copies = []
     size = d.ct * SUB
     for p in range(d.pl):
-        rows[p, SUB - 2] = tail_ref[0, p]
-        rows[p, SUB - 1] = tail_ref[1, p] - HOP * work[3 * STEPS - 3, p, :, : d.cols]
-        loads[p].wait()
-        transpose_tiles(d, 0, p, rows[p], stage)
+        for row in (d.rows - 2, d.rows - 1):
+            above = v[STEPS - 1][row + STEPS + 1, p, :, : d.cols]
+            v[STEPS][row, p] = v[STEPS][row, p] - HOP * above
+        transpose_tiles(d, 0, p, v[STEPS].rows((d.rt - 1) * SUB, SUB)[:, p], stage)
         copies.append(pltpu.make_async_copy(
-            stage.at[p], out_ref.at[:, p, pl.ds((d.rt - 1) * size, size)], osem.at[p]
+            stage.at[p], out_ref.at[:, p, pl.ds((d.rt - 1) * size, size)], sem.at[p]
         ))
         copies[-1].start()
     for copy in copies:
         copy.wait()
 
 
-def green_kernel(d, sites, tables_ref, packed_ref, out_ref):
+def moment_blocks():
+    return [2 * m for m in range(STEPS)] + [2 * m + 1 for m in range(1, STEPS + 1)]
+
+
+def pick_kernel(d, out_ref):
+    column = lax.broadcasted_iota(jnp.int32, (LANES, LANES), 0)
+    lane = lax.broadcasted_iota(jnp.int32, (LANES, LANES), 1)
+    for i, block in enumerate(moment_blocks()):
+        for turned, index in enumerate((lane % d.q, lane // d.q)):
+            hit = (column == block * d.q + index) & (lane < d.q * d.q)
+            out_ref[:, lanes_of(2 * i + turned)] = jnp.where(hit, 1.0, 0.0).astype(jnp.bfloat16)
+
+
+def green_kernel(d, sites, tables_ref, picks_ref, packed_ref, out_ref):
     q = d.q
     rest = packed_ref[...]
     parts = []
@@ -459,33 +450,25 @@
         parts.append(rest.astype(jnp.bfloat16).astype(F32))
         rest = rest - parts[-1]
     left = jnp.concatenate(parts + [jnp.zeros_like(rest)], 0).astype(jnp.bfloat16)
-    column = lax.broadcasted_iota(jnp.int32, (LANES, LANES), 0)
-    lane = lax.broadcasted_iota(jnp.int32, (LANES, LANES), 1)
     sub = lax.broadcasted_iota(jnp.int32, (q, LANES), 0)
     out_lane = lax.broadcasted_iota(jnp.int32, (q, LANES), 1)
-    major, minor = lane // q, lane % q
-    used = lane < q * q
-    blocks = [2 * m for m in range(STEPS)] + [2 * m + 1 for m in range(1, STEPS + 1)]
-    picks = []
-    for block in blocks:
-        for index in (minor, major):
-            hit = (column == block * q + index) & used
-            picks.append(jnp.where(hit, 1.0, 0.0).astype(jnp.bfloat16))
-    wide = jnp.dot(left, jnp.concatenate(picks, 1), preferred_element_type=F32)
+    wide = jnp.dot(left, picks_ref[...], preferred_element_type=F32)
     wide = wide[:q] + wide[q : 2 * q] + wide[2 * q : 3 * q]
     straight, turned = sub == out_lane // q, sub == out_lane % q
     flat = []
-    for i in range(len(blocks)):
+    for i in range(len(moment_blocks())):
         one = jnp.where(straight, wide[:, lanes_of(2 * i)], 0.0)
         two = jnp.where(turned, wide[:, lanes_of(2 * i + 1)], 0.0)
         flat.append(jnp.sum(one + two, 0, keepdims=True) * (0.5 / sites))
     moments = flat[:STEPS]
     for m, base in ((0, 2), (1, 1), (2, 0), (3, 1)):
         moments.append(2.0 * flat[STEPS + m] - moments[base])
-    moments = jnp.concatenate(moments, 0)
+    high, low = split_pair(jnp.concatenate(moments, 0))
+    weight, weight_low = split_pair(tables_ref[...])
+    left = jnp.concatenate([high, high, low, jnp.zeros_like(low)], 0).astype(jnp.bfloat16)
+    right = jnp.concatenate([weight, weight_low, weight, jnp.zeros_like(weight)], 0)
     total = lax.dot_general(
-        moments, tables_ref[...], (((0,), (0,)), ((), ())),
-        precision=lax.Precision.HIGHEST, preferred_element_type=F32,
+        left, right.astype(jnp.bfloat16), (((0,), (0,)), ((), ())), preferred_element_type=F32
     )
     energies = total.shape[1] // 2
     for part in range(2):
@@ -571,28 +554,26 @@
         compiler_params=params(4), name="first",
     )(first_row, first_energy, in_hbm(bits))
     ua = send(ua, "gx", 1)
-    names = ("ub", "da", "db", "dc")
-    v0, ons, *sends, right, left = pl.pallas_call(
+    v0, ons, da, right, left = pl.pallas_call(
         functools.partial(fill_kernel, d),
-        out_shape=[vectors[0], onsite] + [tiles(d.tiles(name)) for name in names]
-        + [tiles(d.edge_tiles)] * 2,
-        in_specs=[SMEM, HBM, HBM], out_specs=[VMEM] * 8,
+        out_shape=[vectors[0], onsite, tiles(d.tiles("da"))] + [tiles(d.edge_tiles)] * 2,
+        in_specs=[SMEM, HBM, HBM], out_specs=[VMEM] * 5,
         scratch_shapes=[
             pltpu.VMEM((d.pl, d.q) + bits.shape[2:], jnp.int32), pltpu.VMEM(levels.shape, jnp.int32),
             dma((d.pl + 1,)),
         ],
         compiler_params=params(6), name="fill",
     )(first_row, in_hbm(bits), levels)
-    ub, da, db, dc = sends
     before = send(right, "gy", 1)
     after = send(left, "gy", -1)
-    v0, ons, ub, da = pl.pallas_call(
+    v0, ons, da, ub, db, dc = pl.pallas_call(
         functools.partial(side_kernel, d),
-        out_shape=[vectors[0], onsite, tiles(d.tiles("ub")), tiles(d.tiles("da"))],
-        in_specs=[VMEM] * 6, out_specs=[VMEM] * 4,
-        input_output_aliases={2: 0, 3: 1, 4: 2, 5: 3},
-        compiler_params=params(2), name="side",
-    )(before, after, v0, ons, ub, da)
+        out_shape=[vectors[0], onsite] + [tiles(d.tiles(name)) for name in ("da", "ub", "db", "dc")],
+        in_specs=[VMEM] * 5, out_specs=[VMEM] * 6,
+        scratch_shapes=[pltpu.VMEM((3, d.pl, d.q, d.width), F32)],
+        input_output_aliases={2: 0, 3: 1, 4: 2},
+        compiler_params=params(3), name="side",
+    )(before, after, v0, ons, da)
     ub = send(ub, "gx", 1)
     da = send(da, "gx", -1)
     db = send(db, "gx", -1)
@@ -620,40 +601,30 @@
         [ua, ub], ("ua", "ub"), every, kept, [pltpu.HBM(bits.shape, F32)], [HBM],
         [pltpu.VMEM((d.pl, d.q, stage_rows, LANES), F32), dma((d.pl,))],
     )
-    block = (SUB, d.pl, d.q, d.cols)
-    *kept, top = wave(
-        [da], ("da",), (("d", 1), ("d", 2)), kept,
-        [pltpu.HBM(block, F32)], [HBM], [dma],
-    )
-    extra = [
-        pltpu.VMEM((2 * (STEPS - 1), d.pl, d.q, d.width), F32),
-        pltpu.VMEM((STEPS - 2, d.pl, d.width), F32),
-        pltpu.VMEM((2,) + block[1:], F32),
-        pltpu.VMEM((d.q, LANES), F32),
-    ]
-    *_, edge, edge_ons, tail, gram = wave([db], ("db",), (("d", 3),), kept, extra, [VMEM] * 4)
+    kept = wave([da], ("da",), (("d", 1), ("d", 2)), kept)
+    *kept, _, gram = wave([db], ("db",), (("d", 3),), kept, [pltpu.VMEM((d.q, LANES), F32)], [VMEM])
     last_vector = pl.pallas_call(
         functools.partial(last_kernel, d),
-        out_shape=jax.ShapeDtypeStruct(bits.shape, F32),
-        in_specs=[VMEM] * 4 + [HBM] * 2, out_specs=HBM,
-        scratch_shapes=[
-            pltpu.VMEM((3 * STEPS - 2, d.pl, d.q, d.width), F32),
-            pltpu.VMEM((STEPS - 1, d.pl, d.width), F32),
-            pltpu.VMEM((d.pl, SUB, d.q, d.cols), F32),
-            pltpu.VMEM((d.pl, d.q, d.ct * SUB, LANES), F32), dma((d.pl,)), dma((d.pl,)),
-        ],
-        input_output_aliases={5: 0},
-        compiler_params=params(9), name="last",
-    )(dc, edge, edge_ons, tail, top, lower)
+        out_shape=[jax.ShapeDtypeStruct(bits.shape, F32)] + kinds[:-1],
+        in_specs=[VMEM] * (len(kept) + 1) + [HBM], out_specs=[HBM] + [VMEM] * len(kept),
+        scratch_shapes=[pltpu.VMEM((d.pl, d.q, d.ct * SUB, LANES), F32), dma((d.pl,))],
+        input_output_aliases={**{1 + i: 1 + i for i in range(len(kept))}, len(kept) + 1: 0},
+        compiler_params=params(4), name="last",
+    )(dc, *kept, lower)[0]
     last_vector = untile_view(last_vector, probe_bits.shape)
 
     gram = add_over(add_over(gram, "gy"), "gx")
     tables = energy_tables(first_energy + jnp.arange(per_device), NMOM, NE)
+    picks = pl.pallas_call(
+        functools.partial(pick_kernel, d),
+        out_shape=[pltpu.VMEM((LANES, 2 * NMOM * LANES), jnp.bfloat16)], out_specs=[VMEM],
+        compiler_params=params(1), name="picks",
+    )()[0]
     green = pl.pallas_call(
         functools.partial(green_kernel, d, sites),
         out_shape=jax.ShapeDtypeStruct((2, d.q * d.q, per_device), F32),
-        in_specs=[VMEM] * 2, out_specs=VMEM, compiler_params=params(2), name="green",
-    )(tables, gram)
+        in_specs=[VMEM] * 3, out_specs=VMEM, compiler_params=params(2), name="green",
+    )(tables, picks, gram)
     return green.transpose(0, 2, 1), last_vector
 
 

time: 82.8 us -> 79.7 us (0.963)
  waiting for transfers between devices: 26.6 us -> 24.4 us
  Pallas kernels: 31.5 us -> 29.6 us
  starting transfers between devices: 16.9 us -> 17.9 us
    ppermute x3, waiting for transfers between devices: 7.14 us -> 5.11 us  [add_over(): lax.ppermute(value, axis, [(i, i ^ shift) for i in range(peers)])]
    pallas_call x3, Pallas kernels: 9.56 us -> 7.77 us  [wave(): pl.pallas_call(functools.partial(wave_kernel, d, names, waves), out_shape...]
    pallas_call x1, Pallas kernels: 0.49 us -> 1.55 us  [on_device(): pl.pallas_call(functools.partial(side_kernel, d), out_shape=[vectors[0],...]
    ppermute x7, waiting for transfers between devices: 19 us -> 17.9 us  [send(): lax.ppermute(array, axis, [(i, (i + step) % peers) for i in range(peers)])]
    pallas_call x1 -> x2, Pallas kernels: 2.53 us -> 1.61 us  [the longest x1 1.51 us: on_device(): pl.pallas_call(functools.partial(last_kernel, d), out_shape=[jax.ShapeDty...]
    ppermute x3, waiting for transfers between devices: 0.46 us -> 1.33 us  [add_over(): lax.ppermute(value, axis, [(i, i ^ s) for i in range(peers)])]
    unnamed x14 -> x12, local copies, waits for them, and re-layouts: 6.58 us -> 6.57 us
  transfers between devices with their start and end apart: 13 -> 13, of which waited for: 6 -> 7; matrix products, arithmetic and copies ran while one was open for 0% -> 0% of each run, Pallas kernels for 32% -> 29%
where the time goes in v1:
time: 79.7 us; the launch traced here: 79.5 us
  Pallas kernels  29.6 us (37%)
  waiting for transfers between devices  24.4 us (31%)
  starting transfers between devices  17.9 us (22%)
  local copies, waits for them, and re-layouts  6.57 us (8%)
    ppermute x7, waiting for transfers between devices, send(): lax.ppermute(array, axis, [(i, (i + step) % peers) for i in range(peers)])  17.9 us
    pallas_call x1, Pallas kernels, on_device(): pl.pallas_call(functools.partial(interior_kernel, d), out_shape=vectors[1...  13 us
    ppermute x7, starting transfers between devices, send(): lax.ppermute(array, axis, [(i, (i + step) % peers) for i in range(peers)])  12.4 us
    pallas_call x3, Pallas kernels, wave(): pl.pallas_call(functools.partial(wave_kernel, d, names, waves), out_shape...  7.77 us
    unnamed x12, local copies, waits for them, and re-layouts  6.57 us
    ppermute x3, waiting for transfers between devices, add_over(): lax.ppermute(value, axis, [(i, i ^ shift) for i in range(peers)])  5.11 us
    ppermute x3, starting transfers between devices, add_over(): lax.ppermute(value, axis, [(i, i ^ s) for i in range(peers)])  3.49 us
    pallas_call x1, Pallas kernels, on_device(): pl.pallas_call(functools.partial(fill_kernel, d), out_shape=[vectors[0],...  2.9 us
  transfers between devices with their start and end apart: 13, of which 7 were waited for; matrix products, arithmetic and copies ran while one was open for 0% of the time, Pallas kernels for 29%

profile of v1, /device:TPU:0, one launch (start us, length us, event | category | flops | bytes accessed | tf_op | source)
XLA Modules:
  0.0 79.5 jit_solution(16227634929495340560)
XLA Ops:
  0.6 2.9 %fill.1 = (f32[24,8,8,1152]{3,2,1,0:T(8,128)S(1)}, f32[24,8,1152]{2,1,0:T(8,128)S(1)}, f32[138,8,128]{2,1,0:T(8,128)S(1)}, f32[5,8,128]{2,1,0:T(8,128)S(1)}, f32[5,8,128]{2,1,0:T(8,128)S(1)}) custom-call(s32[1]{0:T(128)} %bitcast.row_ref.__, s32[8,8,128,128]{3,2,1,0:T(8,128)} %bitcast.18, s32[8,128,128]{2,1,0:T(8,128)} %bitcast.21), custom_call_target="tpu_custom_call" | custom-call | tf_op jit(solution)/shard_map/fill/pallas_call | solution.py:557
  3.5 0.5 collective-permute-start
  4.1 4.1 %collective-permute-start.1 = (f32[5,8,128]{2,1,0:T(8,128)S(1)}, f32[5,8,128]{2,1,0:T(8,128)S(1)}, u32[]{:S(2)}, u32[]{:S(2)}) collective-permute-start(f32[5,8,128]{2,1,0:T(8,128)S(1)} %get-tuple-element.42), channel_id=1, source_target_pairs={{0,7},{1,0},{2,1},{3,2},{4,3},{5,4},{6,5},{7,6},{8,15},{9,8},{10,9... | collective-permute-start | bytes 61448 | tf_op jit(solution)/shard_map/ppermute | solution.py:527
  8.2 1.4 %collective-permute-done.before_ref = f32[5,8,128]{2,1,0:T(8,128)S(1)} collective-permute-done((f32[5,8,128]{2,1,0:T(8,128)S(1)}, f32[5,8,128]{2,1,0:T(8,128)S(1)}, u32[]{:S(2)}, u32[]{:S(2)}) %collective-permute-start) | collective-permute-done | bytes 20512 | tf_op jit(solution)/shard_map/ppermute | solution.py:527
  9.6 0.1 collective-permute-done.1.after_ref
  9.7 1.6 %side.1 = (f32[24,8,8,1152]{3,2,1,0:T(8,128)S(1)}, f32[24,8,1152]{2,1,0:T(8,128)S(1)}, f32[138,8,128]{2,1,0:T(8,128)S(1)}, f32[139,8,128]{2,1,0:T(8,128)S(1)}, f...) custom-call(f32[5,8,128]{2,1,0:T(8,128)S(1)} %collective-permute-don, ...), custom_call_target="tpu_custom_call", output_to_operand_aliasing={{0}: (2, {}), {1}: (3, {}), {2}: (4, {})} | custom-call | tf_op jit(solution)/shard_map/side/pallas_call | solution.py:569
  11.2 0.0 copy-start
  11.2 2.9 %copy-done = f32[24,8,8,1152]{3,2,1,0:T(8,128)} copy-done((f32[24,8,8,1152]{3,2,1,0:T(8,128)}, f32[24,8,8,1152]{3,2,1,0:T(8,128)S(1)}, u32[]{:S(2)}) %copy-start) | copy-done | bytes 7077912
  14.1 0.0 copy-start.3
  14.1 0.7 copy-done.3
  14.8 1.9 %collective-permute-start.5 = (f32[139,8,128]{2,1,0:T(8,128)S(1)}, f32[139,8,128]{2,1,0:T(8,128)S(1)}, u32[]{:S(2)}, u32[]{:S(2)}) collective-permute-start(f32[139,8,128]{2,1,0:T(8,128)S(1)} %get-tuple-element.48), channel_id=1, source_target_pairs={{0,8},{8,16},{16,24},{24,0},{1,9},{9,17},{17,25},{25,1},{2,10},{10... | collective-permute-start | bytes 1708040 | tf_op jit(solution)/shard_map/ppermute | solution.py:527
  16.7 1.0 %collective-permute-start.3 = (f32[138,8,128]{2,1,0:T(8,128)S(1)}, f32[138,8,128]{2,1,0:T(8,128)S(1)}, u32[]{:S(2)}, u32[]{:S(2)}) collective-permute-start(f32[138,8,128]{2,1,0:T(8,128)S(1)} %get-tuple-element.47), channel_id=1, source_target_pairs={{0,24},{8,0},{16,8},{24,16},{1,25},{9,1},{17,9},{25,17},{2,26},{10... | collective-permute-start | bytes 1695752 | tf_op jit(solution)/shard_map/ppermute | solution.py:527
  17.7 1.6 %first.1 = f32[128,8,128]{2,1,0:T(8,128)S(1)} custom-call(s32[1]{0:T(128)} %bitcast.row_ref.__, s32[1]{0:T(128)} %bitcast.7.___, s32[8,8,128,128]{3,2,1,0:T(8,128)} %bitcast.19), custom_call_target="tpu_custom_call" | custom-call | tf_op jit(solution)/shard_map/first/pallas_call | solution.py:550
  19.3 1.1 %collective-permute-start.4 = (f32[128,8,128]{2,1,0:T(8,128)S(1)}, f32[128,8,128]{2,1,0:T(8,128)S(1)}, u32[]{:S(2)}, u32[]{:S(2)}) collective-permute-start(f32[128,8,128]{2,1,0:T(8,128)S(1)} %first.1), channel_id=1, source_target_pairs={{0,8},{8,16},{16,24},{24,0},{1,9},{9,17},{17,25},{25,1},{2,10},{10... | collective-permute-start | bytes 1572872 | tf_op jit(solution)/shard_map/ppermute | solution.py:527
  20.4 1.9 %collective-permute-start.2 = (f32[65,8,128]{2,1,0:T(8,128)S(1)}, f32[65,8,128]{2,1,0:T(8,128)S(1)}, u32[]{:S(2)}, u32[]{:S(2)}) collective-permute-start(f32[65,8,128]{2,1,0:T(8,128)S(1)} %get-tuple-element.46), channel_id=1, source_target_pairs={{0,24},{8,0},{16,8},{24,16},{1,25},{9,1},{17,9},{25,17},{2,26},{10... | collective-permute-start | bytes 798728 | tf_op jit(solution)/shard_map/ppermute | solution.py:527
  22.3 0.0 copy-start.1
  22.3 3.0 %copy-done.1 = f32[24,8,8,1152]{3,2,1,0:T(8,128)S(1)} copy-done((f32[24,8,8,1152]{3,2,1,0:T(8,128)S(1)}, f32[24,8,8,1152]{3,2,1,0:T(8,128)}, u32[]{:S(2)}) %copy-start.1) | copy-done | bytes 7077912
  25.3 0.0 copy-start.2
  25.3 13.0 %interior.1 = (f32[22,8,8,1152]{3,2,1,0:T(8,128)S(1)}, f32[20,8,8,1152]{3,2,1,0:T(8,128)S(1)}, f32[18,8,8,1152]{3,2,1,0:T(8,128)S(1)}, f32[16,8,8,1024]{3,2,1,0:T(8,128)S(1)}, f32[24,128]{1,0:T(8,128)S(1)}) custom-call(f32[24,8,8,1152]{3,2,1,0:T(8,128)S(1)} %copy-done.1, f32[24,8,1152]{2,1,0:T(8,128)S(1)} %get-tuple-element.50.ons.refs_7_), custom_call_target="tpu_custom_call" | custom-call | tf_op jit(solution)/shard_map/interior/pallas_call | solution.py:581
  38.4 16.4 %collective-permute-done.4.refs_0_ = f32[128,8,128]{2,1,0:T(8,128)S(1)} collective-permute-done((f32[128,8,128]{2,1,0:T(8,128)S(1)}, f32[128,8,128]{2,1,0:T(8,128)S(1)}, u32[]{:S(2)}, u32[]{:S(2)}) %collective-permute-start.4) | collective-permute-done | bytes 524320 | tf_op jit(solution)/shard_map/ppermute | solution.py:527
  54.8 0.0 collective-permute-done.5.refs_1_
  54.8 0.0 copy-done.2
  54.8 4.3 %shard_map.50 = (f32[24,8,8,1152]{3,2,1,0:T(8,128)S(1)}, f32[22,8,8,1152]{3,2,1,0:T(8,128)S(1)}, f32[20,8,8,1152]{3,2,1,0:T(8,128)S(1)}, f32[18,8,8,1152]{3,2,1,...) custom-call(f32[128,8,128]{2,1,0:T(8,128)S(1)} %collective-permute-d, ...), custom_call_target="tpu_custom_call", output_to_operand_aliasing={{0}: (2, {}), {1}: (3, {}), {2}: (4, {}), {3}: (5, {}), {4}... | custom-call | tf_op jit(solution)/shard_map/pallas_call | solution.py:590
  59.1 0.0 collective-permute-done.3.refs_0_
  59.1 2.4 %shard_map.51 = (f32[24,8,8,1152]{3,2,1,0:T(8,128)S(1)}, f32[22,8,8,1152]{3,2,1,0:T(8,128)S(1)}, f32[20,8,8,1152]{3,2,1,0:T(8,128)S(1)}, f32[18,8,8,1152]{3,2,1,...) custom-call(f32[138,8,128]{2,1,0:T(8,128)S(1)} %collective-permute-d, ...), custom_call_target="tpu_custom_call", output_to_operand_aliasing={{0}: (1, {}), {1}: (2, {}), {2}: (3, {}), {3}: (4, {}), {4}... | custom-call | tf_op jit(solution)/shard_map/pallas_call | solution.py:590
  61.5 0.0 collective-permute-done.2.refs_0_
  61.5 0.0 copy-start.4
  61.5 0.0 copy-start.5
  61.5 1.1 %shard_map.52 = (f32[24,8,8,1152]{3,2,1,0:T(8,128)S(1)}, f32[22,8,8,1152]{3,2,1,0:T(8,128)S(1)}, f32[20,8,8,1152]{3,2,1,0:T(8,128)S(1)}, f32[18,8,8,1152]{3,2,1,...) custom-call(f32[65,8,128]{2,1,0:T(8,128)S(1)} %collective-permute-do, ...), custom_call_target="tpu_custom_call", output_to_operand_aliasing={{0}: (1, {}), {1}: (2, {}), {2}: (3, {}), {3}: (4, {}), {4}... | custom-call | tf_op jit(solution)/shard_map/pallas_call | solution.py:590
  62.6 0.0 collective-permute-start.6
  62.6 0.1 sqrt_atan2_fusion
  62.8 1.0 %collective-permute-done.6 = f32[8,128]{1,0:T(8,128)S(1)} collective-permute-done((f32[8,128]{1,0:T(8,128)S(1)}, f32[8,128]{1,0:T(8,128)S(1)}, u32[]{:S(2)}, u32[]{:S(2)}) %collective-permute-start.6) | collective-permute-done | bytes 4128 | tf_op jit(solution)/shard_map/ppermute | solution.py:511
  63.8 0.4 collective-permute-start.7
  64.2 0.0 copy-done.4
  64.2 1.8 %collective-permute-start.12 = (f32[64,8,128]{2,1,0:T(8,128)S(1)}, f32[64,8,128]{2,1,0:T(8,128)S(1)}, u32[]{:S(2)}, u32[]{:S(2)}) collective-permute-start(f32[64,8,128]{2,1,0:T(8,128)S(1)} %copy-done.4), channel_id=1, source_target_pairs={{0,24},{8,0},{16,8},{24,16},{1,25},{9,1},{17,9},{25,17},{2,26},{10... | collective-permute-start | bytes 786440 | tf_op jit(solution)/shard_map/ppermute | solution.py:527
  66.0 1.4 %collective-permute-done.7 = f32[8,128]{1,0:T(8,128)S(1)} collective-permute-done((f32[8,128]{1,0:T(8,128)S(1)}, f32[8,128]{1,0:T(8,128)S(1)}, u32[]{:S(2)}, u32[]{:S(2)}) %collective-permute-start.7) | collective-permute-done | bytes 4128 | tf_op jit(solution)/shard_map/ppermute | solution.py:511
  67.4 1.7 %collective-permute-start.8 = (f32[8,128]{1,0:T(8,128)S(1)}, f32[8,128]{1,0:T(8,128)S(1)}, u32[]{:S(2)}, u32[]{:S(2)}) collective-permute-start(f32[8,128]{1,0:T(8,128)S(1)} %add.55), channel_id=1, source_target_pairs={{0,4},{1,5},{2,6},{3,7},{4,0},{5,1},{6,2},{7,3},{8,12},{9,13},{10,... | collective-permute-start | bytes 12296 | tf_op jit(solution)/shard_map/ppermute | solution.py:511
  69.1 0.0 copy-done.5
  69.1 0.1 fusion.1
  69.2 2.7 %collective-permute-done.8 = f32[8,128]{1,0:T(8,128)S(1)} collective-permute-done((f32[8,128]{1,0:T(8,128)S(1)}, f32[8,128]{1,0:T(8,128)S(1)}, u32[]{:S(2)}, u32[]{:S(2)}) %collective-permute-start.8) | collective-permute-done | bytes 4128 | tf_op jit(solution)/shard_map/ppermute | solution.py:511
  71.9 2.0 %collective-permute-start.10 = (f32[8,128]{1,0:T(8,128)S(1)}, f32[8,128]{1,0:T(8,128)S(1)}, u32[]{:S(2)}, u32[]{:S(2)}) collective-permute-start(f32[8,128]{1,0:T(8,128)S(1)} %add.56), channel_id=1, source_target_pairs={{0,16},{8,24},{16,0},{24,8},{1,17},{9,25},{17,1},{25,9},{2,18},{10... | collective-permute-start | bytes 12296 | tf_op jit(solution)/shard_map/ppermute | solution.py:507
  73.9 0.5 collective-permute-start.11
  74.4 1.0 %collective-permute-start.9 = (f32[8,128]{1,0:T(8,128)S(1)}, f32[8,128]{1,0:T(8,128)S(1)}, u32[]{:S(2)}, u32[]{:S(2)}) collective-permute-start(f32[8,128]{1,0:T(8,128)S(1)} %add.56), channel_id=1, source_target_pairs={{0,8},{8,0},{16,24},{24,16},{1,9},{9,1},{17,25},{25,17},{2,10},{10... | collective-permute-start | bytes 12296 | tf_op jit(solution)/shard_map/ppermute | solution.py:507
  75.4 0.1 picks.1.picks_ref
  75.5 0.0 collective-permute-done.12.dc_ref
  75.5 1.5 %last.1 = (f32[8,8,128,128]{3,2,1,0:T(8,128)}, f32[24,8,8,1152]{3,2,1,0:T(8,128)S(1)}, f32[22,8,8,1152]{3,2,1,0:T(8,128)S(1)}, f32[20,8,8,1152]{3,2,1,0:T(8,128)...) custom-call(f32[64,8,128]{2,1,0:T(8,128)S(1)} %collective-permute-do, ...), custom_call_target="tpu_custom_call", output_to_operand_aliasing={{1}: (1, {}), {2}: (2, {}), {3}: (3, {}), {4}: (4, {}), {5}... | custom-call | tf_op jit(solution)/shard_map/last/pallas_call | solution.py:606
  77.1 0.0 collective-permute-done.10
  77.1 1.3 %collective-permute-done.11 = f32[8,128]{1,0:T(8,128)S(1)} collective-permute-done((f32[8,128]{1,0:T(8,128)S(1)}, f32[8,128]{1,0:T(8,128)S(1)}, u32[]{:S(2)}, u32[]{:S(2)}) %collective-permute-start.11) | collective-permute-done | bytes 4128 | tf_op jit(solution)/shard_map/ppermute | solution.py:507
  78.4 0.0 collective-permute-done.9
  78.4 1.1 %green.1 = f32[2,64,256]{2,1,0:T(8,128)} custom-call(f32[8,512]{1,0:T(8,128)S(1)} %pad_maximum_fusion.tables_ref, bf16[128,2048]{1,0:T(8,128)(2,1)S(1)} %picks.1.picks_ref, f32[8,128]{1,0:T(8,128)S(1)} %add_add_fusion.packed_ref), custom_call_target="tpu_custom_call" | custom-call | tf_op jit(solution)/shard_map/green/pallas_call | solution.py:623
  (6 shorter events, 0.0 us)
Async XLA Ops:
  3.5 6.0 %collective-permute-start = (f32[5,8,128]{2,1,0:T(8,128)S(1)}, f32[5,8,128]{2,1,0:T(8,128)S(1)}, u32[]{:S(2)}, u32[]{:S(2)}) collective-permute-start(f32[5,8,128]{2,1,0:T(8,128)S(1)} %get-tuple-element.41), channel_id=1, source_target_pairs={{0,1},{1,2},{2,3},{3,4},{4,5},{5,6},{6,7},{7,0},{8,9},{9,10},{10,1... | collective-permute-start | bytes 61448 | tf_op jit(solution)/shard_map/ppermute | solution.py:527
  4.1 5.6 %collective-permute-start.1 = (f32[5,8,128]{2,1,0:T(8,128)S(1)}, f32[5,8,128]{2,1,0:T(8,128)S(1)}, u32[]{:S(2)}, u32[]{:S(2)}) collective-permute-start(f32[5,8,128]{2,1,0:T(8,128)S(1)} %get-tuple-element.42), channel_id=1, source_target_pairs={{0,7},{1,0},{2,1},{3,2},{4,3},{5,4},{6,5},{7,6},{8,15},{9,8},{10,9... | collective-permute-start | bytes 61448 | tf_op jit(solution)/shard_map/ppermute | solution.py:527
  11.2 2.9 %copy-start = (f32[24,8,8,1152]{3,2,1,0:T(8,128)}, f32[24,8,8,1152]{3,2,1,0:T(8,128)S(1)}, u32[]{:S(2)}) copy-start(f32[24,8,8,1152]{3,2,1,0:T(8,128)S(1)} %get-tuple-element.49.v_ref.refs_2_) | copy-start | bytes 21233668
  14.1 0.7 copy-start.3
  14.8 40.0 %collective-permute-start.5 = (f32[139,8,128]{2,1,0:T(8,128)S(1)}, f32[139,8,128]{2,1,0:T(8,128)S(1)}, u32[]{:S(2)}, u32[]{:S(2)}) collective-permute-start(f32[139,8,128]{2,1,0:T(8,128)S(1)} %get-tuple-element.48), channel_id=1, source_target_pairs={{0,8},{8,16},{16,24},{24,0},{1,9},{9,17},{17,25},{25,1},{2,10},{10... | collective-permute-start | bytes 1708040 | tf_op jit(solution)/shard_map/ppermute | solution.py:527
  16.7 42.4 %collective-permute-start.3 = (f32[138,8,128]{2,1,0:T(8,128)S(1)}, f32[138,8,128]{2,1,0:T(8,128)S(1)}, u32[]{:S(2)}, u32[]{:S(2)}) collective-permute-start(f32[138,8,128]{2,1,0:T(8,128)S(1)} %get-tuple-element.47), channel_id=1, source_target_pairs={{0,24},{8,0},{16,8},{24,16},{1,25},{9,1},{17,9},{25,17},{2,26},{10... | collective-permute-start | bytes 1695752 | tf_op jit(solution)/shard_map/ppermute | solution.py:527
  19.3 35.5 %collective-permute-start.4 = (f32[128,8,128]{2,1,0:T(8,128)S(1)}, f32[128,8,128]{2,1,0:T(8,128)S(1)}, u32[]{:S(2)}, u32[]{:S(2)}) collective-permute-start(f32[128,8,128]{2,1,0:T(8,128)S(1)} %first.1), channel_id=1, source_target_pairs={{0,8},{8,16},{16,24},{24,0},{1,9},{9,17},{17,25},{25,1},{2,10},{10... | collective-permute-start | bytes 1572872 | tf_op jit(solution)/shard_map/ppermute | solution.py:527
  20.4 41.1 %collective-permute-start.2 = (f32[65,8,128]{2,1,0:T(8,128)S(1)}, f32[65,8,128]{2,1,0:T(8,128)S(1)}, u32[]{:S(2)}, u32[]{:S(2)}) collective-permute-start(f32[65,8,128]{2,1,0:T(8,128)S(1)} %get-tuple-element.46), channel_id=1, source_target_pairs={{0,24},{8,0},{16,8},{24,16},{1,25},{9,1},{17,9},{25,17},{2,26},{10... | collective-permute-start | bytes 798728 | tf_op jit(solution)/shard_map/ppermute | solution.py:527
  22.3 3.0 %copy-start.1 = (f32[24,8,8,1152]{3,2,1,0:T(8,128)S(1)}, f32[24,8,8,1152]{3,2,1,0:T(8,128)}, u32[]{:S(2)}) copy-start(f32[24,8,8,1152]{3,2,1,0:T(8,128)} %copy-done) | copy-start | bytes 21233668
  25.3 29.5 %copy-start.2 = (f32[24,8,8,1152]{3,2,1,0:T(8,128)S(1)}, f32[24,8,8,1152]{3,2,1,0:T(8,128)}, u32[]{:S(2)}) copy-start(f32[24,8,8,1152]{3,2,1,0:T(8,128)} %copy-done) | copy-start | bytes 21233668
  61.5 2.7 %copy-start.4 = (f32[64,8,128]{2,1,0:T(8,128)S(1)}, f32[64,8,128]{2,1,0:T(8,128)}, u32[]{:S(2)}) copy-start(f32[64,8,128]{2,1,0:T(8,128)} %copy-done.3) | copy-start | bytes 786436
  61.5 7.6 %copy-start.5 = (f32[8]{0:T(128)S(1)}, f32[8]{0:T(128)}, u32[]{:S(2)}) copy-start(f32[8]{0:T(128)} %constant.29) | copy-start | bytes 100
  62.6 1.2 %collective-permute-start.6 = (f32[8,128]{1,0:T(8,128)S(1)}, f32[8,128]{1,0:T(8,128)S(1)}, u32[]{:S(2)}, u32[]{:S(2)}) collective-permute-start(f32[8,128]{1,0:T(8,128)S(1)} %get-tuple-element.70), channel_id=1, source_target_pairs={{0,1},{1,0},{2,3},{3,2},{4,5},{5,4},{6,7},{7,6},{8,9},{9,8},{10,11... | collective-permute-start | bytes 12296 | tf_op jit(solution)/shard_map/ppermute | solution.py:511
  63.8 3.6 %collective-permute-start.7 = (f32[8,128]{1,0:T(8,128)S(1)}, f32[8,128]{1,0:T(8,128)S(1)}, u32[]{:S(2)}, u32[]{:S(2)}) collective-permute-start(f32[8,128]{1,0:T(8,128)S(1)} %add.54), channel_id=1, source_target_pairs={{0,2},{1,3},{2,0},{3,1},{4,6},{5,7},{6,4},{7,5},{8,10},{9,11},{10,... | collective-permute-start | bytes 12296 | tf_op jit(solution)/shard_map/ppermute | solution.py:511
  64.2 11.3 %collective-permute-start.12 = (f32[64,8,128]{2,1,0:T(8,128)S(1)}, f32[64,8,128]{2,1,0:T(8,128)S(1)}, u32[]{:S(2)}, u32[]{:S(2)}) collective-permute-start(f32[64,8,128]{2,1,0:T(8,128)S(1)} %copy-done.4), channel_id=1, source_target_pairs={{0,24},{8,0},{16,8},{24,16},{1,25},{9,1},{17,9},{25,17},{2,26},{10... | collective-permute-start | bytes 786440 | tf_op jit(solution)/shard_map/ppermute | solution.py:527
  67.4 4.5 %collective-permute-start.8 = (f32[8,128]{1,0:T(8,128)S(1)}, f32[8,128]{1,0:T(8,128)S(1)}, u32[]{:S(2)}, u32[]{:S(2)}) collective-permute-start(f32[8,128]{1,0:T(8,128)S(1)} %add.55), channel_id=1, source_target_pairs={{0,4},{1,5},{2,6},{3,7},{4,0},{5,1},{6,2},{7,3},{8,12},{9,13},{10,... | collective-permute-start | bytes 12296 | tf_op jit(solution)/shard_map/ppermute | solution.py:511
  71.9 5.1 %collective-permute-start.10 = (f32[8,128]{1,0:T(8,128)S(1)}, f32[8,128]{1,0:T(8,128)S(1)}, u32[]{:S(2)}, u32[]{:S(2)}) collective-permute-start(f32[8,128]{1,0:T(8,128)S(1)} %add.56), channel_id=1, source_target_pairs={{0,16},{8,24},{16,0},{24,8},{1,17},{9,25},{17,1},{25,9},{2,18},{10... | collective-permute-start | bytes 12296 | tf_op jit(solution)/shard_map/ppermute | solution.py:507
  73.9 4.5 %collective-permute-start.11 = (f32[8,128]{1,0:T(8,128)S(1)}, f32[8,128]{1,0:T(8,128)S(1)}, u32[]{:S(2)}, u32[]{:S(2)}) collective-permute-start(f32[8,128]{1,0:T(8,128)S(1)} %add.56), channel_id=1, source_target_pairs={{0,24},{8,16},{16,8},{24,0},{1,25},{9,17},{17,9},{25,1},{2,26},{10... | collective-permute-start | bytes 12296 | tf_op jit(solution)/shard_map/ppermute | solution.py:507
  74.4 4.0 %collective-permute-start.9 = (f32[8,128]{1,0:T(8,128)S(1)}, f32[8,128]{1,0:T(8,128)S(1)}, u32[]{:S(2)}, u32[]{:S(2)}) collective-permute-start(f32[8,128]{1,0:T(8,128)S(1)} %add.56), channel_id=1, source_target_pairs={{0,8},{8,0},{16,24},{24,16},{1,9},{9,1},{17,25},{25,17},{2,10},{10... | collective-permute-start | bytes 12296 | tf_op jit(solution)/shard_map/ppermute | solution.py:507

commit v2 on v1

--- a/solution.py
+++ b/solution.py
@@ -367,8 +367,13 @@
         at_of = lambda n: STEPS + n - k if side == "u" else top - (n - k)
         if k == STEPS:
             complete(d, side, v)
-        for n in range(max(1, k - 1), STEPS):
-            one_row(d, n, at_of(n), v, ons)
+        if side == "d" and k == STEPS - 1:
+            for n in range(2, STEPS):
+                for p in range(d.pl):
+                    v[n][at_of(n), p] = v[n][at_of(n), p] - HOP * v[n - 1][at_of(n - 1), p]
+        else:
+            for n in range(max(1, k - 1), STEPS):
+                one_row(d, n, at_of(n), v, ons)
         at = at_of(STEPS)
         if side == "u" or k < STEPS - 1:
             one_row(d, STEPS, at, v, ons)
@@ -377,6 +382,10 @@
     if ("u", STEPS) in waves:
         flush(d, v[STEPS], *extra)
     if ("d", STEPS - 2) in waves:
+        for n in range(2, STEPS):
+            at = top + STEPS - 1 - n
+            for p, value in enumerate(row_values(d, n, at, v, ons, leave=at + 1)):
+                v[n][at, p] = value
         for p, value in enumerate(row_values(d, STEPS, top - 1, v, ons, leave=top)):
             v[STEPS][d.rows - 2, p] = value[:, : d.cols]
         gram(top - 1)

time: 79.7 us -> 79.6 us (level)
  no operation moved by 1% of the time
where the time goes in v2:
time: 79.6 us; the launch traced here: 79.4 us
  Pallas kernels  29.5 us (37%)
  waiting for transfers between devices  24.3 us (31%)
  starting transfers between devices  17.9 us (22%)
  local copies, waits for them, and re-layouts  6.57 us (8%)
    ppermute x7, waiting for transfers between devices, send(): lax.ppermute(array, axis, [(i, (i + step) % peers) for i in range(peers)])  17.9 us
    pallas_call x1, Pallas kernels, on_device(): pl.pallas_call(functools.partial(interior_kernel, d), out_shape=vectors[1...  13 us
    ppermute x7, starting transfers between devices, send(): lax.ppermute(array, axis, [(i, (i + step) % peers) for i in range(peers)])  12.4 us
    pallas_call x3, Pallas kernels, wave(): pl.pallas_call(functools.partial(wave_kernel, d, names, waves), out_shape...  7.74 us
    unnamed x12, local copies, waits for them, and re-layouts  6.57 us
    ppermute x3, waiting for transfers between devices, add_over(): lax.ppermute(value, axis, [(i, i ^ shift) for i in range(peers)])  5.11 us
    ppermute x3, starting transfers between devices, add_over(): lax.ppermute(value, axis, [(i, i ^ s) for i in range(peers)])  3.49 us
    pallas_call x1, Pallas kernels, on_device(): pl.pallas_call(functools.partial(fill_kernel, d), out_shape=[vectors[0],...  2.9 us
  transfers between devices with their start and end apart: 13, of which 7 were waited for; matrix products, arithmetic and copies ran while one was open for 0% of the time, Pallas kernels for 29%

profile of v2, /device:TPU:0, one launch (start us, length us, event | category | flops | bytes accessed | tf_op | source)
XLA Modules:
  0.0 79.4 jit_solution(9411931866868641252)
XLA Ops:
  0.6 2.9 %fill.1 = (f32[24,8,8,1152]{3,2,1,0:T(8,128)S(1)}, f32[24,8,1152]{2,1,0:T(8,128)S(1)}, f32[138,8,128]{2,1,0:T(8,128)S(1)}, f32[5,8,128]{2,1,0:T(8,128)S(1)}, f32[5,8,128]{2,1,0:T(8,128)S(1)}) custom-call(s32[1]{0:T(128)} %bitcast.row_ref.__, s32[8,8,128,128]{3,2,1,0:T(8,128)} %bitcast.18, s32[8,128,128]{2,1,0:T(8,128)} %bitcast.21), custom_call_target="tpu_custom_call" | custom-call | tf_op jit(solution)/shard_map/fill/pallas_call | solution.py:566
  3.5 0.5 collective-permute-start
  4.1 4.1 %collective-permute-start.1 = (f32[5,8,128]{2,1,0:T(8,128)S(1)}, f32[5,8,128]{2,1,0:T(8,128)S(1)}, u32[]{:S(2)}, u32[]{:S(2)}) collective-permute-start(f32[5,8,128]{2,1,0:T(8,128)S(1)} %get-tuple-element.42), channel_id=1, source_target_pairs={{0,7},{1,0},{2,1},{3,2},{4,3},{5,4},{6,5},{7,6},{8,15},{9,8},{10,9... | collective-permute-start | bytes 61448 | tf_op jit(solution)/shard_map/ppermute | solution.py:536
  8.2 1.4 %collective-permute-done.before_ref = f32[5,8,128]{2,1,0:T(8,128)S(1)} collective-permute-done((f32[5,8,128]{2,1,0:T(8,128)S(1)}, f32[5,8,128]{2,1,0:T(8,128)S(1)}, u32[]{:S(2)}, u32[]{:S(2)}) %collective-permute-start) | collective-permute-done | bytes 20512 | tf_op jit(solution)/shard_map/ppermute | solution.py:536
  9.6 0.1 collective-permute-done.1.after_ref
  9.7 1.6 %side.1 = (f32[24,8,8,1152]{3,2,1,0:T(8,128)S(1)}, f32[24,8,1152]{2,1,0:T(8,128)S(1)}, f32[138,8,128]{2,1,0:T(8,128)S(1)}, f32[139,8,128]{2,1,0:T(8,128)S(1)}, f...) custom-call(f32[5,8,128]{2,1,0:T(8,128)S(1)} %collective-permute-don, ...), custom_call_target="tpu_custom_call", output_to_operand_aliasing={{0}: (2, {}), {1}: (3, {}), {2}: (4, {})} | custom-call | tf_op jit(solution)/shard_map/side/pallas_call | solution.py:578
  11.2 0.0 copy-start
  11.2 2.9 %copy-done = f32[24,8,8,1152]{3,2,1,0:T(8,128)} copy-done((f32[24,8,8,1152]{3,2,1,0:T(8,128)}, f32[24,8,8,1152]{3,2,1,0:T(8,128)S(1)}, u32[]{:S(2)}) %copy-start) | copy-done | bytes 7077912
  14.1 0.0 copy-start.3
  14.1 0.7 copy-done.3
  14.8 1.9 %collective-permute-start.5 = (f32[139,8,128]{2,1,0:T(8,128)S(1)}, f32[139,8,128]{2,1,0:T(8,128)S(1)}, u32[]{:S(2)}, u32[]{:S(2)}) collective-permute-start(f32[139,8,128]{2,1,0:T(8,128)S(1)} %get-tuple-element.48), channel_id=1, source_target_pairs={{0,8},{8,16},{16,24},{24,0},{1,9},{9,17},{17,25},{25,1},{2,10},{10... | collective-permute-start | bytes 1708040 | tf_op jit(solution)/shard_map/ppermute | solution.py:536
  16.7 1.0 %collective-permute-start.3 = (f32[138,8,128]{2,1,0:T(8,128)S(1)}, f32[138,8,128]{2,1,0:T(8,128)S(1)}, u32[]{:S(2)}, u32[]{:S(2)}) collective-permute-start(f32[138,8,128]{2,1,0:T(8,128)S(1)} %get-tuple-element.47), channel_id=1, source_target_pairs={{0,24},{8,0},{16,8},{24,16},{1,25},{9,1},{17,9},{25,17},{2,26},{10... | collective-permute-start | bytes 1695752 | tf_op jit(solution)/shard_map/ppermute | solution.py:536
  17.7 1.6 %first.1 = f32[128,8,128]{2,1,0:T(8,128)S(1)} custom-call(s32[1]{0:T(128)} %bitcast.row_ref.__, s32[1]{0:T(128)} %bitcast.7.___, s32[8,8,128,128]{3,2,1,0:T(8,128)} %bitcast.19), custom_call_target="tpu_custom_call" | custom-call | tf_op jit(solution)/shard_map/first/pallas_call | solution.py:559
  19.3 1.1 %collective-permute-start.4 = (f32[128,8,128]{2,1,0:T(8,128)S(1)}, f32[128,8,128]{2,1,0:T(8,128)S(1)}, u32[]{:S(2)}, u32[]{:S(2)}) collective-permute-start(f32[128,8,128]{2,1,0:T(8,128)S(1)} %first.1), channel_id=1, source_target_pairs={{0,8},{8,16},{16,24},{24,0},{1,9},{9,17},{17,25},{25,1},{2,10},{10... | collective-permute-start | bytes 1572872 | tf_op jit(solution)/shard_map/ppermute | solution.py:536
  20.4 1.9 %collective-permute-start.2 = (f32[65,8,128]{2,1,0:T(8,128)S(1)}, f32[65,8,128]{2,1,0:T(8,128)S(1)}, u32[]{:S(2)}, u32[]{:S(2)}) collective-permute-start(f32[65,8,128]{2,1,0:T(8,128)S(1)} %get-tuple-element.46), channel_id=1, source_target_pairs={{0,24},{8,0},{16,8},{24,16},{1,25},{9,1},{17,9},{25,17},{2,26},{10... | collective-permute-start | bytes 798728 | tf_op jit(solution)/shard_map/ppermute | solution.py:536
  22.3 0.0 copy-start.1
  22.3 3.0 %copy-done.1 = f32[24,8,8,1152]{3,2,1,0:T(8,128)S(1)} copy-done((f32[24,8,8,1152]{3,2,1,0:T(8,128)S(1)}, f32[24,8,8,1152]{3,2,1,0:T(8,128)}, u32[]{:S(2)}) %copy-start.1) | copy-done | bytes 7077912
  25.3 0.0 copy-start.2
  25.3 13.0 %interior.1 = (f32[22,8,8,1152]{3,2,1,0:T(8,128)S(1)}, f32[20,8,8,1152]{3,2,1,0:T(8,128)S(1)}, f32[18,8,8,1152]{3,2,1,0:T(8,128)S(1)}, f32[16,8,8,1024]{3,2,1,0:T(8,128)S(1)}, f32[24,128]{1,0:T(8,128)S(1)}) custom-call(f32[24,8,8,1152]{3,2,1,0:T(8,128)S(1)} %copy-done.1, f32[24,8,1152]{2,1,0:T(8,128)S(1)} %get-tuple-element.50.ons.refs_7_), custom_call_target="tpu_custom_call" | custom-call | tf_op jit(solution)/shard_map/interior/pallas_call | solution.py:590
  38.4 16.4 %collective-permute-done.4.refs_0_ = f32[128,8,128]{2,1,0:T(8,128)S(1)} collective-permute-done((f32[128,8,128]{2,1,0:T(8,128)S(1)}, f32[128,8,128]{2,1,0:T(8,128)S(1)}, u32[]{:S(2)}, u32[]{:S(2)}) %collective-permute-start.4) | collective-permute-done | bytes 524320 | tf_op jit(solution)/shard_map/ppermute | solution.py:536
  54.8 0.0 collective-permute-done.5.refs_1_
  54.8 0.0 copy-done.2
  54.8 4.3 %shard_map.50 = (f32[24,8,8,1152]{3,2,1,0:T(8,128)S(1)}, f32[22,8,8,1152]{3,2,1,0:T(8,128)S(1)}, f32[20,8,8,1152]{3,2,1,0:T(8,128)S(1)}, f32[18,8,8,1152]{3,2,1,...) custom-call(f32[128,8,128]{2,1,0:T(8,128)S(1)} %collective-permute-d, ...), custom_call_target="tpu_custom_call", output_to_operand_aliasing={{0}: (2, {}), {1}: (3, {}), {2}: (4, {}), {3}: (5, {}), {4}... | custom-call | tf_op jit(solution)/shard_map/pallas_call | solution.py:599
  59.1 0.0 collective-permute-done.3.refs_0_
  59.1 2.6 %shard_map.51 = (f32[24,8,8,1152]{3,2,1,0:T(8,128)S(1)}, f32[22,8,8,1152]{3,2,1,0:T(8,128)S(1)}, f32[20,8,8,1152]{3,2,1,0:T(8,128)S(1)}, f32[18,8,8,1152]{3,2,1,...) custom-call(f32[138,8,128]{2,1,0:T(8,128)S(1)} %collective-permute-d, ...), custom_call_target="tpu_custom_call", output_to_operand_aliasing={{0}: (1, {}), {1}: (2, {}), {2}: (3, {}), {3}: (4, {}), {4}... | custom-call | tf_op jit(solution)/shard_map/pallas_call | solution.py:599
  61.7 0.0 collective-permute-done.2.refs_0_
  61.7 0.0 copy-start.4
  61.7 0.0 copy-start.5
  61.7 0.8 %shard_map.52 = (f32[24,8,8,1152]{3,2,1,0:T(8,128)S(1)}, f32[22,8,8,1152]{3,2,1,0:T(8,128)S(1)}, f32[20,8,8,1152]{3,2,1,0:T(8,128)S(1)}, f32[18,8,8,1152]{3,2,1,...) custom-call(f32[65,8,128]{2,1,0:T(8,128)S(1)} %collective-permute-do, ...), custom_call_target="tpu_custom_call", output_to_operand_aliasing={{0}: (1, {}), {1}: (2, {}), {2}: (3, {}), {3}: (4, {}), {4}... | custom-call | tf_op jit(solution)/shard_map/pallas_call | solution.py:599
  62.6 0.0 collective-permute-start.6
  62.6 0.1 sqrt_atan2_fusion
  62.7 1.0 %collective-permute-done.6 = f32[8,128]{1,0:T(8,128)S(1)} collective-permute-done((f32[8,128]{1,0:T(8,128)S(1)}, f32[8,128]{1,0:T(8,128)S(1)}, u32[]{:S(2)}, u32[]{:S(2)}) %collective-permute-start.6) | collective-permute-done | bytes 4128 | tf_op jit(solution)/shard_map/ppermute | solution.py:520
  63.8 0.4 collective-permute-start.7
  64.2 0.0 copy-done.4
  64.2 1.8 %collective-permute-start.12 = (f32[64,8,128]{2,1,0:T(8,128)S(1)}, f32[64,8,128]{2,1,0:T(8,128)S(1)}, u32[]{:S(2)}, u32[]{:S(2)}) collective-permute-start(f32[64,8,128]{2,1,0:T(8,128)S(1)} %copy-done.4), channel_id=1, source_target_pairs={{0,24},{8,0},{16,8},{24,16},{1,25},{9,1},{17,9},{25,17},{2,26},{10... | collective-permute-start | bytes 786440 | tf_op jit(solution)/shard_map/ppermute | solution.py:536
  66.0 1.4 %collective-permute-done.7 = f32[8,128]{1,0:T(8,128)S(1)} collective-permute-done((f32[8,128]{1,0:T(8,128)S(1)}, f32[8,128]{1,0:T(8,128)S(1)}, u32[]{:S(2)}, u32[]{:S(2)}) %collective-permute-start.7) | collective-permute-done | bytes 4128 | tf_op jit(solution)/shard_map/ppermute | solution.py:520
  67.4 1.7 %collective-permute-start.8 = (f32[8,128]{1,0:T(8,128)S(1)}, f32[8,128]{1,0:T(8,128)S(1)}, u32[]{:S(2)}, u32[]{:S(2)}) collective-permute-start(f32[8,128]{1,0:T(8,128)S(1)} %add.55), channel_id=1, source_target_pairs={{0,4},{1,5},{2,6},{3,7},{4,0},{5,1},{6,2},{7,3},{8,12},{9,13},{10,... | collective-permute-start | bytes 12296 | tf_op jit(solution)/shard_map/ppermute | solution.py:520
  69.1 0.0 copy-done.5
  69.1 0.1 fusion.1
  69.2 2.7 %collective-permute-done.8 = f32[8,128]{1,0:T(8,128)S(1)} collective-permute-done((f32[8,128]{1,0:T(8,128)S(1)}, f32[8,128]{1,0:T(8,128)S(1)}, u32[]{:S(2)}, u32[]{:S(2)}) %collective-permute-start.8) | collective-permute-done | bytes 4128 | tf_op jit(solution)/shard_map/ppermute | solution.py:520
  71.9 2.0 %collective-permute-start.10 = (f32[8,128]{1,0:T(8,128)S(1)}, f32[8,128]{1,0:T(8,128)S(1)}, u32[]{:S(2)}, u32[]{:S(2)}) collective-permute-start(f32[8,128]{1,0:T(8,128)S(1)} %add.56), channel_id=1, source_target_pairs={{0,16},{8,24},{16,0},{24,8},{1,17},{9,25},{17,1},{25,9},{2,18},{10... | collective-permute-start | bytes 12296 | tf_op jit(solution)/shard_map/ppermute | solution.py:516
  73.9 0.5 collective-permute-start.11
  74.4 1.0 %collective-permute-start.9 = (f32[8,128]{1,0:T(8,128)S(1)}, f32[8,128]{1,0:T(8,128)S(1)}, u32[]{:S(2)}, u32[]{:S(2)}) collective-permute-start(f32[8,128]{1,0:T(8,128)S(1)} %add.56), channel_id=1, source_target_pairs={{0,8},{8,0},{16,24},{24,16},{1,9},{9,1},{17,25},{25,17},{2,10},{10... | collective-permute-start | bytes 12296 | tf_op jit(solution)/shard_map/ppermute | solution.py:516
  75.4 0.1 picks.1.picks_ref
  75.5 0.0 collective-permute-done.12.dc_ref
  75.5 1.5 %last.1 = (f32[8,8,128,128]{3,2,1,0:T(8,128)}, f32[24,8,8,1152]{3,2,1,0:T(8,128)S(1)}, f32[22,8,8,1152]{3,2,1,0:T(8,128)S(1)}, f32[20,8,8,1152]{3,2,1,0:T(8,128)...) custom-call(f32[64,8,128]{2,1,0:T(8,128)S(1)} %collective-permute-do, ...), custom_call_target="tpu_custom_call", output_to_operand_aliasing={{1}: (1, {}), {2}: (2, {}), {3}: (3, {}), {4}: (4, {}), {5}... | custom-call | tf_op jit(solution)/shard_map/last/pallas_call | solution.py:615
  77.0 0.0 collective-permute-done.10
  77.0 1.3 %collective-permute-done.11 = f32[8,128]{1,0:T(8,128)S(1)} collective-permute-done((f32[8,128]{1,0:T(8,128)S(1)}, f32[8,128]{1,0:T(8,128)S(1)}, u32[]{:S(2)}, u32[]{:S(2)}) %collective-permute-start.11) | collective-permute-done | bytes 4128 | tf_op jit(solution)/shard_map/ppermute | solution.py:516
  78.4 0.0 collective-permute-done.9
  78.4 1.1 %green.1 = f32[2,64,256]{2,1,0:T(8,128)} custom-call(f32[8,512]{1,0:T(8,128)S(1)} %pad_maximum_fusion.tables_ref, bf16[128,2048]{1,0:T(8,128)(2,1)S(1)} %picks.1.picks_ref, f32[8,128]{1,0:T(8,128)S(1)} %add_add_fusion.packed_ref), custom_call_target="tpu_custom_call" | custom-call | tf_op jit(solution)/shard_map/green/pallas_call | solution.py:632
  (6 shorter events, 0.0 us)
Async XLA Ops:
  3.5 6.0 %collective-permute-start = (f32[5,8,128]{2,1,0:T(8,128)S(1)}, f32[5,8,128]{2,1,0:T(8,128)S(1)}, u32[]{:S(2)}, u32[]{:S(2)}) collective-permute-start(f32[5,8,128]{2,1,0:T(8,128)S(1)} %get-tuple-element.41), channel_id=1, source_target_pairs={{0,1},{1,2},{2,3},{3,4},{4,5},{5,6},{6,7},{7,0},{8,9},{9,10},{10,1... | collective-permute-start | bytes 61448 | tf_op jit(solution)/shard_map/ppermute | solution.py:536
  4.1 5.6 %collective-permute-start.1 = (f32[5,8,128]{2,1,0:T(8,128)S(1)}, f32[5,8,128]{2,1,0:T(8,128)S(1)}, u32[]{:S(2)}, u32[]{:S(2)}) collective-permute-start(f32[5,8,128]{2,1,0:T(8,128)S(1)} %get-tuple-element.42), channel_id=1, source_target_pairs={{0,7},{1,0},{2,1},{3,2},{4,3},{5,4},{6,5},{7,6},{8,15},{9,8},{10,9... | collective-permute-start | bytes 61448 | tf_op jit(solution)/shard_map/ppermute | solution.py:536
  11.2 2.9 %copy-start = (f32[24,8,8,1152]{3,2,1,0:T(8,128)}, f32[24,8,8,1152]{3,2,1,0:T(8,128)S(1)}, u32[]{:S(2)}) copy-start(f32[24,8,8,1152]{3,2,1,0:T(8,128)S(1)} %get-tuple-element.49.v_ref.refs_2_) | copy-start | bytes 21233668
  14.1 0.7 copy-start.3
  14.8 40.0 %collective-permute-start.5 = (f32[139,8,128]{2,1,0:T(8,128)S(1)}, f32[139,8,128]{2,1,0:T(8,128)S(1)}, u32[]{:S(2)}, u32[]{:S(2)}) collective-permute-start(f32[139,8,128]{2,1,0:T(8,128)S(1)} %get-tuple-element.48), channel_id=1, source_target_pairs={{0,8},{8,16},{16,24},{24,0},{1,9},{9,17},{17,25},{25,1},{2,10},{10... | collective-permute-start | bytes 1708040 | tf_op jit(solution)/shard_map/ppermute | solution.py:536
  16.7 42.4 %collective-permute-start.3 = (f32[138,8,128]{2,1,0:T(8,128)S(1)}, f32[138,8,128]{2,1,0:T(8,128)S(1)}, u32[]{:S(2)}, u32[]{:S(2)}) collective-permute-start(f32[138,8,128]{2,1,0:T(8,128)S(1)} %get-tuple-element.47), channel_id=1, source_target_pairs={{0,24},{8,0},{16,8},{24,16},{1,25},{9,1},{17,9},{25,17},{2,26},{10... | collective-permute-start | bytes 1695752 | tf_op jit(solution)/shard_map/ppermute | solution.py:536
  19.3 35.5 %collective-permute-start.4 = (f32[128,8,128]{2,1,0:T(8,128)S(1)}, f32[128,8,128]{2,1,0:T(8,128)S(1)}, u32[]{:S(2)}, u32[]{:S(2)}) collective-permute-start(f32[128,8,128]{2,1,0:T(8,128)S(1)} %first.1), channel_id=1, source_target_pairs={{0,8},{8,16},{16,24},{24,0},{1,9},{9,17},{17,25},{25,1},{2,10},{10... | collective-permute-start | bytes 1572872 | tf_op jit(solution)/shard_map/ppermute | solution.py:536
  20.4 41.3 %collective-permute-start.2 = (f32[65,8,128]{2,1,0:T(8,128)S(1)}, f32[65,8,128]{2,1,0:T(8,128)S(1)}, u32[]{:S(2)}, u32[]{:S(2)}) collective-permute-start(f32[65,8,128]{2,1,0:T(8,128)S(1)} %get-tuple-element.46), channel_id=1, source_target_pairs={{0,24},{8,0},{16,8},{24,16},{1,25},{9,1},{17,9},{25,17},{2,26},{10... | collective-permute-start | bytes 798728 | tf_op jit(solution)/shard_map/ppermute | solution.py:536
  22.3 3.0 %copy-start.1 = (f32[24,8,8,1152]{3,2,1,0:T(8,128)S(1)}, f32[24,8,8,1152]{3,2,1,0:T(8,128)}, u32[]{:S(2)}) copy-start(f32[24,8,8,1152]{3,2,1,0:T(8,128)} %copy-done) | copy-start | bytes 21233668
  25.3 29.5 %copy-start.2 = (f32[24,8,8,1152]{3,2,1,0:T(8,128)S(1)}, f32[24,8,8,1152]{3,2,1,0:T(8,128)}, u32[]{:S(2)}) copy-start(f32[24,8,8,1152]{3,2,1,0:T(8,128)} %copy-done) | copy-start | bytes 21233668
  61.7 2.4 %copy-start.4 = (f32[64,8,128]{2,1,0:T(8,128)S(1)}, f32[64,8,128]{2,1,0:T(8,128)}, u32[]{:S(2)}) copy-start(f32[64,8,128]{2,1,0:T(8,128)} %copy-done.3) | copy-start | bytes 786436
  61.7 7.3 %copy-start.5 = (f32[8]{0:T(128)S(1)}, f32[8]{0:T(128)}, u32[]{:S(2)}) copy-start(f32[8]{0:T(128)} %constant.29) | copy-start | bytes 100
  62.6 1.2 %collective-permute-start.6 = (f32[8,128]{1,0:T(8,128)S(1)}, f32[8,128]{1,0:T(8,128)S(1)}, u32[]{:S(2)}, u32[]{:S(2)}) collective-permute-start(f32[8,128]{1,0:T(8,128)S(1)} %get-tuple-element.70), channel_id=1, source_target_pairs={{0,1},{1,0},{2,3},{3,2},{4,5},{5,4},{6,7},{7,6},{8,9},{9,8},{10,11... | collective-permute-start | bytes 12296 | tf_op jit(solution)/shard_map/ppermute | solution.py:520
  63.8 3.6 %collective-permute-start.7 = (f32[8,128]{1,0:T(8,128)S(1)}, f32[8,128]{1,0:T(8,128)S(1)}, u32[]{:S(2)}, u32[]{:S(2)}) collective-permute-start(f32[8,128]{1,0:T(8,128)S(1)} %add.54), channel_id=1, source_target_pairs={{0,2},{1,3},{2,0},{3,1},{4,6},{5,7},{6,4},{7,5},{8,10},{9,11},{10,... | collective-permute-start | bytes 12296 | tf_op jit(solution)/shard_map/ppermute | solution.py:520
  64.2 11.3 %collective-permute-start.12 = (f32[64,8,128]{2,1,0:T(8,128)S(1)}, f32[64,8,128]{2,1,0:T(8,128)S(1)}, u32[]{:S(2)}, u32[]{:S(2)}) collective-permute-start(f32[64,8,128]{2,1,0:T(8,128)S(1)} %copy-done.4), channel_id=1, source_target_pairs={{0,24},{8,0},{16,8},{24,16},{1,25},{9,1},{17,9},{25,17},{2,26},{10... | collective-permute-start | bytes 786440 | tf_op jit(solution)/shard_map/ppermute | solution.py:536
  67.4 4.5 %collective-permute-start.8 = (f32[8,128]{1,0:T(8,128)S(1)}, f32[8,128]{1,0:T(8,128)S(1)}, u32[]{:S(2)}, u32[]{:S(2)}) collective-permute-start(f32[8,128]{1,0:T(8,128)S(1)} %add.55), channel_id=1, source_target_pairs={{0,4},{1,5},{2,6},{3,7},{4,0},{5,1},{6,2},{7,3},{8,12},{9,13},{10,... | collective-permute-start | bytes 12296 | tf_op jit(solution)/shard_map/ppermute | solution.py:520
  71.9 5.1 %collective-permute-start.10 = (f32[8,128]{1,0:T(8,128)S(1)}, f32[8,128]{1,0:T(8,128)S(1)}, u32[]{:S(2)}, u32[]{:S(2)}) collective-permute-start(f32[8,128]{1,0:T(8,128)S(1)} %add.56), channel_id=1, source_target_pairs={{0,16},{8,24},{16,0},{24,8},{1,17},{9,25},{17,1},{25,9},{2,18},{10... | collective-permute-start | bytes 12296 | tf_op jit(solution)/shard_map/ppermute | solution.py:516
  73.9 4.5 %collective-permute-start.11 = (f32[8,128]{1,0:T(8,128)S(1)}, f32[8,128]{1,0:T(8,128)S(1)}, u32[]{:S(2)}, u32[]{:S(2)}) collective-permute-start(f32[8,128]{1,0:T(8,128)S(1)} %add.56), channel_id=1, source_target_pairs={{0,24},{8,16},{16,8},{24,0},{1,25},{9,17},{17,9},{25,1},{2,26},{10... | collective-permute-start | bytes 12296 | tf_op jit(solution)/shard_map/ppermute | solution.py:516
  74.4 4.0 %collective-permute-start.9 = (f32[8,128]{1,0:T(8,128)S(1)}, f32[8,128]{1,0:T(8,128)S(1)}, u32[]{:S(2)}, u32[]{:S(2)}) collective-permute-start(f32[8,128]{1,0:T(8,128)S(1)} %add.56), channel_id=1, source_target_pairs={{0,8},{8,0},{16,24},{24,16},{1,9},{9,1},{17,25},{25,17},{2,10},{10... | collective-permute-start | bytes 12296 | tf_op jit(solution)/shard_map/ppermute | solution.py:516
